TPU v7x, 32 devices: a whole 2x2x4 slice. The times are simulated.
32 devices in a mesh: groups: 2 (over x), col: 16 (over z, y, core).
Axes of the slice: x: 2, y: 2, z: 4, core: 2. Of those that a mesh axis runs over, the one named last changes fastest.
Arguments:
- slab: float32 [2, 2048, 4096], P(None, 'groups', 'col'), parts along dimension 1, may hold values from -6 to 6
- block_on: int32 [16, 32], P('groups', 'col'), parts along dimension 0, may hold values 0 or 1
- block_band: int32 [16, 32], P('groups', 'col'), parts along dimension 0, may hold values from 0 to 3
- band_gain: float32 [4], replicated, may hold values from 0.25 to 2
Outputs:
- spectra: float32 [2, 2048, 4096], P(None, 'groups', 'col'), parts along dimension 1
There are 2 independent parts, one for each index of `groups`. A program takes and returns all parts, laid end to end along the dimension named above; an argument that names none is the same for every part. Nothing has to cross between parts.
All inputs are finite; a program needn't handle non-finite values. No bound on the sum of `block_on` on one device may be relied on, other than what follows from the above.
Results may differ from a plain program's by a relative error of at most 0.00007.
Values sent between devices are 32-bit elements; how exact they have to be, the bound alone decides.
No kernel may reach another device: no remote copies, remote signals or barrier semaphores. Data moves between devices by JAX's collectives and lax.ppermute only.
A program may use at most 64 MiB of HBM per device.

v0:
```python
import functools
import math

import jax
import jax.numpy as jnp
from jax import lax
from jax.experimental import pallas as pl
from jax.experimental.pallas import tpu as pltpu
from jax.sharding import PartitionSpec as P


BLOCK = 128
SUB = 8
LANES = 128


def phase_table(first_index, second_index, length):
    product = first_index[:, None] * second_index[None, :] % length
    angles = product.astype(jnp.float32) * (2.0 * math.pi / length)
    return (jnp.cos(angles), -jnp.sin(angles))


def contract(stacked, table, formula):
    cosine_table, sine_table = table
    ein = functools.partial(jnp.einsum, formula, precision=lax.Precision.HIGHEST)
    real_part = ein(stacked[0], cosine_table) - ein(stacked[1], sine_table)
    imag_part = ein(stacked[0], sine_table) + ein(stacked[1], cosine_table)
    return jnp.stack([real_part, imag_part])


def rotate(stacked, table):
    cosine_table, sine_table = table
    real_part = stacked[0] * cosine_table - stacked[1] * sine_table
    imag_part = stacked[0] * sine_table + stacked[1] * cosine_table
    return jnp.stack([real_part, imag_part])


def block_weights(block_on, block_band, band_gain, length):
    choose = (block_band[..., None] == jnp.arange(band_gain.shape[0], dtype=jnp.int32)).astype(
        jnp.float32
    )
    factor = 1.0 / math.sqrt(length)
    return block_on.astype(jnp.float32) * jnp.sum(choose * band_gain, axis=-1) * factor


def shards_generic(slab, block_on, block_band, band_gain):
    devices = lax.axis_size("col")
    rows_total, shard_cols = slab.shape[1:]
    length = shard_cols * devices
    rows_here = rows_total // devices
    first_len = BLOCK
    second_len = length // first_len
    first_iota = jnp.arange(first_len, dtype=jnp.int32)
    second_iota = jnp.arange(second_len, dtype=jnp.int32)
    table_one = phase_table(first_iota, first_iota, first_len)
    table_middle = phase_table(first_iota, second_iota, length)
    table_two = phase_table(second_iota, second_iota, second_len)
    received = lax.all_to_all(
        slab.reshape(2, devices, rows_here, shard_cols), "col", split_axis=1, concat_axis=3, tiled=True
    )
    square = received[:, 0].reshape(2, rows_here, first_len, second_len)
    mixture = rotate(contract(square, table_one, "rab,ak->rkb"), table_middle)
    whole = contract(mixture, table_two, "rkb,bm->rmk").reshape(2, rows_here, devices, shard_cols)
    spectrum = lax.all_to_all(whole, "col", split_axis=2, concat_axis=1, tiled=True)
    weight = block_weights(block_on, block_band, band_gain, length)
    blocked = spectrum.reshape(2, rows_total // BLOCK, BLOCK, shard_cols // BLOCK, BLOCK)
    return (blocked * weight[None, :, None, :, None]).reshape(2, rows_total, shard_cols)


def travel_order(devices):
    return sorted(range(devices), key=lambda hop: (-hop.bit_length(), hop))


def pack_all_kernel(first, blocks, slab_ref, out_ref, sem):
    halves = slab_ref.shape[4] // LANES
    copies = []
    for plane in range(2):
        for block in range(blocks):
            for half in range(halves):
                copies.append(
                    pltpu.make_async_copy(
                        slab_ref.at[plane, first + block, :, :, half * LANES : (half + 1) * LANES],
                        out_ref.at[:, (plane * halves + half) * blocks + block],
                        sem.at[len(copies)],
                    )
                )
    for copy in copies:
        copy.start()
    for copy in copies:
        copy.wait()


def pack_each_kernel(first, blocks, me_ref, slab_ref, mask_ref, *refs):
    outs, (stage_ref, in_sem, out_sem) = refs[:-3], refs[-3:]
    halves = slab_ref.shape[4] // LANES
    me = me_ref[0]
    gathers, puts = [], []
    for number, hop in enumerate(travel_order(len(outs))):
        for plane in range(2):
            for half in range(halves):
                tile = (plane * halves + half) * blocks
                lanes = slice(half * LANES, (half + 1) * LANES)
                gathers.append(
                    pltpu.make_async_copy(
                        slab_ref.at[plane, first : first + blocks, me ^ hop, :, lanes],
                        stage_ref.at[number, tile : tile + blocks],
                        in_sem.at[len(gathers)],
                    )
                )
    for copy in gathers:
        copy.start()
    for number in range(len(outs)):
        stage_ref[number, 2 * halves * blocks] = mask_ref[...]
    for number, out in enumerate(outs):
        for copy in gathers[number * 2 * halves : (number + 1) * 2 * halves]:
            copy.wait()
        puts.append(pltpu.make_async_copy(stage_ref.at[number], out, out_sem.at[number]))
        puts[-1].start()
    for copy in puts:
        copy.wait()


def butterflies(parts, length):
    if length == 1:
        return parts
    even = butterflies(parts[0::2], length // 2)
    odd = butterflies(parts[1::2], length // 2)
    low, high = [], []
    for index in range(length // 2):
        even_re, even_im = even[index]
        odd_re, odd_im = odd[index]
        if index == 0:
            turn_re, turn_im = odd_re, odd_im
        elif 4 * index == length:
            turn_re, turn_im = odd_im, -odd_re
        elif 8 * index == length:
            root = math.sqrt(0.5)
            turn_re, turn_im = (odd_re + odd_im) * root, (odd_im - odd_re) * root
        elif 8 * index == 3 * length:
            root = math.sqrt(0.5)
            turn_re, turn_im = (odd_im - odd_re) * root, (odd_re + odd_im) * -root
        else:
            angle = 2.0 * math.pi * index / length
            cosine, sine = math.cos(angle), math.sin(angle)
            turn_re = odd_re * cosine + odd_im * sine
            turn_im = odd_im * cosine - odd_re * sine
        low.append((even_re + turn_re, even_im + turn_im))
        high.append((even_re - turn_re, even_im - turn_im))
    return low + high


def slots_kernel(tiles, bounds, sources, index_ref, place_ref, branch_ref):
    count = len(sources)
    flags = jnp.concatenate([source[source.shape[0] - 1, 0:1] for source in sources], axis=0)
    live = flags > 0.5
    lane = lax.broadcasted_iota(jnp.int32, (count, LANES), 1)
    row = lax.broadcasted_iota(jnp.int32, (LANES, LANES), 0)
    column = lax.broadcasted_iota(jnp.int32, (LANES, LANES), 1)
    ones = jnp.where(live, 1.0, 0.0)
    rank = jnp.dot(
        ones.astype(jnp.bfloat16),
        jnp.where(row < column, 1.0, 0.0).astype(jnp.bfloat16),
        preferred_element_type=jnp.float32,
    ).astype(jnp.int32)
    place = jnp.where(live, rank, LANES)
    index = jnp.zeros((count, LANES), jnp.int32)
    for tile in range(tiles):
        index = jnp.where(place[:, tile : tile + 1] == lane, tile, index)
    index_ref[...] = index
    place_ref[...] = rank
    most = jnp.max(jnp.sum(ones, axis=1, keepdims=True)).astype(jnp.int32)
    branch_ref[0] = sum((most > bound).astype(jnp.int32) for bound in bounds)


def transform_kernel(devices, blocks, masks, table_ref, twiddle_ref, *refs):
    sources, (high_ref, low_ref, mid_ref) = refs[: -7 if masks else -4], refs[-3:]
    out_ref = refs[len(sources)]
    if masks:
        slots_kernel(*masks, sources, *refs[len(sources) + 1 : len(sources) + 4])
    halves = 2
    width = halves * LANES
    bits = devices.bit_length() - 1
    lane = lax.broadcasted_iota(jnp.int32, (2 * SUB, LANES), 1)

    place = travel_order(devices)

    def tile_of(dev, plane, block, half):
        if len(sources) == 1:
            return sources[0][dev, (plane * halves + half) * blocks + block]
        return sources[place.index(dev)][(plane * halves + half) * blocks + block]

    @pl.loop(0, blocks // 2)
    def _(pair):
        for plane in range(2):
            for half in range(halves):
                vals = [
                    jnp.concatenate(
                        [
                            tile_of(dev, plane, pair * 2, half),
                            tile_of(dev, plane, pair * 2 + 1, half),
                        ],
                        axis=0,
                    )
                    for dev in range(devices)
                ]
                for bit in range(bits):
                    step = 1 << bit
                    odd_lane = (lane & step) != 0
                    for dev in range(devices):
                        if dev & step:
                            continue
                        first, second = vals[dev], vals[dev | step]
                        vals[dev] = jnp.where(odd_lane, pltpu.roll(second, step, 1), first)
                        vals[dev | step] = jnp.where(
                            odd_lane, second, pltpu.roll(first, LANES - step, 1)
                        )
                where = slice(plane * width + half * LANES, plane * width + (half + 1) * LANES)
                for dev in range(devices):
                    high = vals[dev].astype(jnp.bfloat16)
                    low = (vals[dev] - high.astype(jnp.float32)).astype(jnp.bfloat16)
                    high_ref[dev, pl.ds(pair * 2 * SUB, 2 * SUB), where] = high
                    low_ref[dev, pl.ds(pair * 2 * SUB, 2 * SUB), where] = low

    rows = blocks * SUB
    dot = functools.partial(jnp.dot, preferred_element_type=jnp.float32)
    lhs_high = high_ref[...].reshape(devices * rows, 2 * width)
    lhs_low = low_ref[...].reshape(devices * rows, 2 * width)
    for plane in range(2):
        columns = slice(plane * width, (plane + 1) * width)
        table = table_ref[:, columns]
        table_high = table.astype(jnp.bfloat16)
        table_low = (table - table_high.astype(jnp.float32)).astype(jnp.bfloat16)
        total = dot(lhs_high, table_high) + (dot(lhs_high, table_low) + dot(lhs_low, table_high))
        mid_ref[:, :, columns] = total.reshape(devices, rows, width)

    @pl.loop(0, blocks)
    def _(block):
        for half in range(halves):
            parts = []
            for dev in range(devices):
                re = mid_ref[dev, pl.ds(block * SUB, SUB), half * LANES : (half + 1) * LANES]
                im = mid_ref[
                    dev, pl.ds(block * SUB, SUB), width + half * LANES : width + (half + 1) * LANES
                ]
                if dev:
                    cosine = twiddle_ref[dev : dev + 1, half * LANES : (half + 1) * LANES]
                    sine = twiddle_ref[dev : dev + 1, width + half * LANES : width + (half + 1) * LANES]
                    re, im = re * cosine + im * sine, im * cosine - re * sine
                parts.append((re, im))
            for dev, (re, im) in enumerate(butterflies(parts, devices)):
                out_ref[dev, block * halves + half, 0] = re
                out_ref[dev, block * halves + half, 1] = im


def compact_kernel(slots, me_ref, index_ref, first_ref, second_ref, *outs):
    split = first_ref.shape[1]
    me = me_ref[0]
    for number, (hop, out) in enumerate(zip(travel_order(len(outs)), outs)):
        dev = me ^ hop
        for slot in range(slots):
            index = index_ref[number, slot]
            early = first_ref[dev, jnp.minimum(index, split - 1)]
            late = second_ref[dev, jnp.maximum(index - split, 0)]
            out[slot] = jnp.where(index < split, early, late)


def spread_kernel(devices, me_ref, slot_ref, weight_ref, *refs):
    sources, (out_ref, stage_ref, sem) = refs[:-3], refs[-3:]
    halves = out_ref.shape[2] // LANES
    blocks = out_ref.shape[1] // BLOCK
    last = sources[0].shape[0] - 1
    me = me_ref[0]

    def copy_of(block):
        rows = pl.ds(pl.multiple_of(block * BLOCK, BLOCK), BLOCK)
        return pltpu.make_async_copy(stage_ref.at[:, rows], out_ref.at[:, rows], sem.at[block])

    @pl.loop(0, blocks)
    def _(block):
        for half in range(halves):
            slot = jnp.minimum(slot_ref[block * halves + half], last)
            weight = weight_ref[block * halves + half]
            for number, hop in enumerate(travel_order(devices)):
                row = pl.multiple_of(block * BLOCK + (me ^ hop) * SUB, SUB)
                for plane in range(2):
                    stage_ref[plane, pl.ds(row, SUB), half * LANES : (half + 1) * LANES] = (
                        sources[number][slot, plane] * weight
                    )
        copy_of(block).start()

    @pl.loop(0, blocks)
    def _(block):
        copy_of(block).wait()


VMEM_SPEC = pl.BlockSpec(memory_space=pltpu.VMEM)
SMEM_SPEC = pl.BlockSpec(memory_space=pltpu.SMEM)
ANY_SPEC = pl.BlockSpec(memory_space=pl.ANY)
HBM_SPEC = pl.BlockSpec(memory_space=pltpu.HBM)
PIECE_SPEC = HBM_SPEC


def shards_tiled(slab, block_on, block_band, band_gain):
    devices = lax.axis_size("col")
    rows_total, shard_cols = slab.shape[1:]
    length = shard_cols * devices
    blocks = rows_total // BLOCK
    halves = shard_cols // LANES
    tiles = blocks * halves
    width = shard_cols
    part = blocks * 3 // 4
    early = part * halves
    me = lax.axis_index("col").astype(jnp.int32).reshape(1)

    def call(body, out_shape, in_specs, scratch=(), cost=None, out_spec=VMEM_SPEC, mib=14):
        many = isinstance(out_shape, list)
        return pl.pallas_call(
            body,
            out_shape=out_shape,
            in_specs=in_specs,
            out_specs=[
                SMEM_SPEC if out.shape == (1,) else out_spec for out in out_shape
            ]
            if many
            else out_spec,
            scratch_shapes=scratch,
            compiler_params=pltpu.CompilerParams(vmem_limit_bytes=mib << 20),
            cost_estimate=cost,
        )

    def trade(values):
        traded = []
        for hop, value in zip(travel_order(devices), values):
            pairs = [(dev, dev ^ hop) for dev in range(devices)]
            traded.append(lax.ppermute(value, "col", pairs) if hop else value)
        return traded

    def shape(*dims):
        return jax.ShapeDtypeStruct(dims, jnp.float32)

    dealt = slab.reshape(2, blocks, devices, SUB, shard_cols)
    flags = jnp.zeros((SUB, LANES), jnp.float32)
    flags = flags.at[0, :tiles].set(block_on.reshape(tiles).astype(jnp.float32))
    pieces = call(
        functools.partial(pack_each_kernel, 0, part),
        [shape(2 * early + 1, SUB, LANES)] * devices,
        [SMEM_SPEC, HBM_SPEC, VMEM_SPEC],
        [
            pltpu.VMEM((devices, 2 * early + 1, SUB, LANES), jnp.float32),
            pltpu.SemaphoreType.DMA((devices * 2 * halves,)),
            pltpu.SemaphoreType.DMA((devices,)),
        ],
        out_spec=PIECE_SPEC,
    )(me, dealt, flags)
    arrived = trade(pieces)
    message = call(
        functools.partial(pack_all_kernel, part, blocks - part),
        shape(devices, 2 * (tiles - early), SUB, LANES),
        [HBM_SPEC],
        [pltpu.SemaphoreType.DMA((2 * (tiles - early),))],
    )(dealt)
    received = lax.all_to_all(message, "col", split_axis=0, concat_axis=0, tiled=True)

    lane = jnp.arange(width, dtype=jnp.int32)

    def square(shift):
        point = ((lane % devices) ^ shift) * (width // devices) + lane // devices
        cosine, minus_sine = phase_table(point, lane, width)
        return jnp.concatenate(
            [
                jnp.concatenate([cosine, minus_sine], axis=1),
                jnp.concatenate([-minus_sine, cosine], axis=1),
            ],
            axis=0,
        )

    cosine, minus_sine = phase_table(jnp.arange(devices, dtype=jnp.int32), lane, length)
    twiddle = jnp.concatenate([cosine, -minus_sine], axis=1)

    capacities = sorted({max(1, tiles * step // 16) for step in (8, 10, 11, 12, 13, 14, 16)})

    def transform(count, masks, table, sources):
        scratch = (devices, count * SUB, 2 * width)
        outs = [shape(devices, count * halves, 2, SUB, LANES)]
        if masks:
            outs += [
                jax.ShapeDtypeStruct((devices, LANES), jnp.int32),
                jax.ShapeDtypeStruct((devices, LANES), jnp.int32),
                jax.ShapeDtypeStruct((1,), jnp.int32),
            ]
        return call(
            functools.partial(transform_kernel, devices, count, masks),
            outs,
            [VMEM_SPEC] * (2 + len(sources)),
            [
                pltpu.VMEM(scratch, jnp.bfloat16),
                pltpu.VMEM(scratch, jnp.bfloat16),
                pltpu.VMEM(scratch, jnp.float32),
            ],
            cost=pl.CostEstimate(
                flops=6 * devices * count * SUB * 4 * width * width,
                bytes_accessed=16 << 20,
                transcendentals=0,
            ),
        )(table, twiddle, *sources)

    weight = block_weights(block_on, block_band, band_gain, length).reshape(tiles)

    first, index, place, branch = transform(part, (tiles, capacities[:-1]), square(me[0]), arrived)
    own_place = place[devices - 1, :tiles]
    (second,) = transform(blocks - part, (), square(0), [received])

    def finish(capacity):
        def run(me, index, own_place, weight, first, second):
            sent = call(
                functools.partial(compact_kernel, capacity),
                [shape(capacity, 2, SUB, LANES)] * devices,
                [SMEM_SPEC, SMEM_SPEC, VMEM_SPEC, VMEM_SPEC],
            )(me, index, first, second)
            return call(
                functools.partial(spread_kernel, devices),
                shape(*slab.shape),
                [SMEM_SPEC] * 3 + [VMEM_SPEC] * devices,
                [pltpu.VMEM(slab.shape, jnp.float32), pltpu.SemaphoreType.DMA((blocks,))],
                out_spec=HBM_SPEC,
            )(me, own_place, weight, *trade(sent))

        return run

    branches = [finish(c) for c in capacities]
    return branch[0], branches, (me, index, own_place, weight, first, second)


def shards(slab, block_on, block_band, band_gain):
    devices = lax.axis_size("col")
    rows_total, shard_cols = slab.shape[1:]
    power = devices & (devices - 1) == 0
    fits = (
        power
        and 2 <= devices <= 32
        and devices * SUB == BLOCK
        and shard_cols == 2 * LANES
        and rows_total % (4 * BLOCK) == 0
        and rows_total // BLOCK * 2 <= LANES
    )
    if fits:
        branch, branches, operands = shards_tiled(slab, block_on, block_band, band_gain)
        return lax.switch(branch, branches, *operands)
    return shards_generic(slab, block_on, block_band, band_gain)


def solution(mesh):
    placed = (P(None, "groups", "col"), P("groups", "col"), P("groups", "col"), P())
    return jax.shard_map(
        shards, mesh=mesh, in_specs=placed, out_specs=P(None, "groups", "col"), check_vma=False
    )
```

profile of v0, /device:TPU:13, one launch (start us, length us, event | category | flops | bytes accessed | tf_op | source)
XLA Modules:
  0.0 123.5 jit_solution(12242421162128570226)
XLA Ops:
  0.0 1.6 %copy-done = f32[2,1024,256]{2,1,0:T(8,128)S(1)} copy-done((f32[2,1024,256]{2,1,0:T(8,128)S(1)}, f32[2,1024,256]{2,1,0:T(8,128)}, u32[]{:S(2)}) %copy-start) | copy-done | bytes 2097176
  2.6 6.5 %all-to-all-start = ((f32[16,8,8,128]{3,2,1,0:T(8,128)}), f32[16,8,8,128]{3,2,1,0:T(8,128)S(1)}, u32[]{:S(2)}, u32[]{:S(2)}) async-start(f32[16,8,8,128]{3,2,1,0:T(8,128)} %shard_map.69), calls=%async_computation | async-start | bytes 1048576 | tf_op jit(solution)/shard_map/all_to_all | solution.py:362
  9.3 3.5 %shard_map.67 = (f32[25,8,128]{2,1,0:T(8,128)S(1)}, f32[25,8,128]{2,1,0:T(8,128)S(1)}, f32[25,8,128]{2,1,0:T(8,128)S(1)}, f32[25,8,128]{2,1,0:T(8,128)S(1)}, f32...) custom-call(s32[1]{0:T(128)} %bitcast.7.me_ref, ...), custom_call_target="tpu_custom_call" | custom-call | tf_op jit(solution)/shard_map/pallas_call | solution.py:344
  12.8 2.2 %collective-permute-start.105 = (f32[25,8,128]{2,1,0:T(8,128)S(1)}, f32[25,8,128]{2,1,0:T(8,128)S(1)}, u32[]{:S(2)}, u32[]{:S(2)}) collective-permute-start(f32[25,8,128]{2,1,0:T(8,128)S(1)} %get-tuple-element.283), channel_id=1, source_target_pairs={{0,8},{1,9},{2,10},{3,11},{4,12},{5,13},{6,14},{7,15},{8,0},{9,1},... | collective-permute-start | bytes 307208 | tf_op jit(solution)/shard_map/ppermute | solution.py:335
  15.8 2.1 %collective-permute-start.107 = (f32[25,8,128]{2,1,0:T(8,128)S(1)}, f32[25,8,128]{2,1,0:T(8,128)S(1)}, u32[]{:S(2)}, u32[]{:S(2)}) collective-permute-start(f32[25,8,128]{2,1,0:T(8,128)S(1)} %get-tuple-element.285), channel_id=1, source_target_pairs={{0,10},{1,11},{2,8},{3,9},{4,14},{5,15},{6,12},{7,13},{8,2},{9,3},... | collective-permute-start | bytes 307208 | tf_op jit(solution)/shard_map/ppermute | solution.py:335
  22.7 11.1 %collective-permute-done.105.refs_0_ = f32[25,8,128]{2,1,0:T(8,128)S(1)} collective-permute-done((f32[25,8,128]{2,1,0:T(8,128)S(1)}, f32[25,8,128]{2,1,0:T(8,128)S(1)}, u32[]{:S(2)}, u32[]{:S(2)}) %collective-permute-start.105) | collective-permute-done | bytes 102432 | tf_op jit(solution)/shard_map/ppermute | solution.py:335
  33.8 2.5 %collective-permute-start.110 = (f32[25,8,128]{2,1,0:T(8,128)S(1)}, f32[25,8,128]{2,1,0:T(8,128)S(1)}, u32[]{:S(2)}, u32[]{:S(2)}) collective-permute-start(f32[25,8,128]{2,1,0:T(8,128)S(1)} %get-tuple-element.288), channel_id=1, source_target_pairs={{0,13},{1,12},{2,15},{3,14},{4,9},{5,8},{6,11},{7,10},{8,5},{9,4},... | collective-permute-start | bytes 307208 | tf_op jit(solution)/shard_map/ppermute | solution.py:335
  38.1 2.4 %collective-permute-start.112 = (f32[25,8,128]{2,1,0:T(8,128)S(1)}, f32[25,8,128]{2,1,0:T(8,128)S(1)}, u32[]{:S(2)}, u32[]{:S(2)}) collective-permute-start(f32[25,8,128]{2,1,0:T(8,128)S(1)} %get-tuple-element.290), channel_id=1, source_target_pairs={{0,15},{1,14},{2,13},{3,12},{4,11},{5,10},{6,9},{7,8},{8,7},{9,6},... | collective-permute-start | bytes 307208 | tf_op jit(solution)/shard_map/ppermute | solution.py:335
  40.5 4.2 %collective-permute-done.108.refs_3_ = f32[25,8,128]{2,1,0:T(8,128)S(1)} collective-permute-done((f32[25,8,128]{2,1,0:T(8,128)S(1)}, f32[25,8,128]{2,1,0:T(8,128)S(1)}, u32[]{:S(2)}, u32[]{:S(2)}) %collective-permute-start.108) | collective-permute-done | bytes 102432 | tf_op jit(solution)/shard_map/ppermute | solution.py:335
  44.7 4.2 %collective-permute-start.113 = (f32[25,8,128]{2,1,0:T(8,128)S(1)}, f32[25,8,128]{2,1,0:T(8,128)S(1)}, u32[]{:S(2)}, u32[]{:S(2)}) collective-permute-start(f32[25,8,128]{2,1,0:T(8,128)S(1)} %get-tuple-element.291), channel_id=1, source_target_pairs={{0,4},{1,5},{2,6},{3,7},{4,0},{5,1},{6,2},{7,3},{8,12},{9,13},{10,... | collective-permute-start | bytes 307208 | tf_op jit(solution)/shard_map/ppermute | solution.py:335
  49.9 4.3 %collective-permute-done.110.refs_5_ = f32[25,8,128]{2,1,0:T(8,128)S(1)} collective-permute-done((f32[25,8,128]{2,1,0:T(8,128)S(1)}, f32[25,8,128]{2,1,0:T(8,128)S(1)}, u32[]{:S(2)}, u32[]{:S(2)}) %collective-permute-start.110) | collective-permute-done | bytes 102432 | tf_op jit(solution)/shard_map/ppermute | solution.py:335
  55.9 2.4 %collective-permute-done.112.refs_7_ = f32[25,8,128]{2,1,0:T(8,128)S(1)} collective-permute-done((f32[25,8,128]{2,1,0:T(8,128)S(1)}, f32[25,8,128]{2,1,0:T(8,128)S(1)}, u32[]{:S(2)}, u32[]{:S(2)}) %collective-permute-start.112) | collective-permute-done | bytes 102432 | tf_op jit(solution)/shard_map/ppermute | solution.py:335
  58.4 2.0 %collective-permute-start.117 = (f32[25,8,128]{2,1,0:T(8,128)S(1)}, f32[25,8,128]{2,1,0:T(8,128)S(1)}, u32[]{:S(2)}, u32[]{:S(2)}) collective-permute-start(f32[25,8,128]{2,1,0:T(8,128)S(1)} %get-tuple-element.295), channel_id=1, source_target_pairs={{0,2},{1,3},{2,0},{3,1},{4,6},{5,7},{6,4},{7,5},{8,10},{9,11},{10,... | collective-permute-start | bytes 307208 | tf_op jit(solution)/shard_map/ppermute | solution.py:335
  62.0 2.6 %collective-permute-done.117.refs_12_ = f32[25,8,128]{2,1,0:T(8,128)S(1)} collective-permute-done((f32[25,8,128]{2,1,0:T(8,128)S(1)}, f32[25,8,128]{2,1,0:T(8,128)S(1)}, u32[]{:S(2)}, u32[]{:S(2)}) %collective-permute-start.117) | collective-permute-done | bytes 102432 | tf_op jit(solution)/shard_map/ppermute | solution.py:335
  64.6 2.2 %collective-permute-done.118.refs_13_ = f32[25,8,128]{2,1,0:T(8,128)S(1)} collective-permute-done((f32[25,8,128]{2,1,0:T(8,128)S(1)}, f32[25,8,128]{2,1,0:T(8,128)S(1)}, u32[]{:S(2)}, u32[]{:S(2)}) %collective-permute-start.118) | collective-permute-done | bytes 102432 | tf_op jit(solution)/shard_map/ppermute | solution.py:335
  66.8 6.4 %shard_map.68 = (f32[16,12,2,8,128]{4,3,2,1,0:T(8,128)}, s32[16,128]{1,0:T(8,128)S(1)}, s32[16,128]{1,0:T(8,128)S(1)}, s32[1]{0:T(128)}) custom-call(f32[512,512]{1,0:T(8,128)S(1)} %maximum_maximum_fusion.table_ref, f32[16,512]{1,0:T(8,128)S(1)} %pad_maximum_fusion.twiddle_ref, f32[25,8,128]{2,1,0:T(8,128)S(1)} %collective-permute-done.105.refs_0_, ...), custom_call_target="tpu_custom_call" | custom-call | flops 1207959552 | bytes 16777216 | tf_op jit(solution)/shard_map/pallas_call | solution.py:391
  73.9 1.3 %shard_map.70 = f32[16,4,2,8,128]{4,3,2,1,0:T(8,128)S(1)} custom-call(f32[512,512]{1,0:T(8,128)S(1)} %maximum_maximum_fusion.1.table_ref, f32[16,512]{1,0:T(8,128)S(1)} %pad_maximum_fusion.twiddle_ref, f32[16,8,8,128]{3,2,1,0:T(8,128)S(1)} %all-to-all-done.refs_0_), custom_call_target="tpu_custom_call" | custom-call | flops 402653184 | bytes 16777216 | tf_op jit(solution)/shard_map/pallas_call | solution.py:391
  75.3 48.0 %conditional.1 = (f32[2,1024,256]{2,1,0:T(8,128)}) conditional(s32[]{:T(128)} %bitcast.9, (s32[1]{0:T(128)}, s32[16,128]{1,0:T(8,128)S(1)}, f32[16,12,2,8,128]{4,3,2,1,0:T(8,128)S(1)}, f32[16,4,2,8,128]{4,3,2,1,0:T(8,128)S(1)}, s32[16,128]{1,0:T(8,128)S(1)}, /*index=5*/f32[8,2]{0,1:T(2,128)S(1)}, (), ...), branch_computations={%region_1.2_spmd, %region_2.3_spmd, %region_3.4_spmd, %region_4.5_... | conditional | flops 208 | bytes 7865912 | solution.py:448
  75.4 1.5 %branch_3_fun.2 = (f32[12,2,8,128]{3,2,1,0:T(8,128)S(1)}, f32[12,2,8,128]{3,2,1,0:T(8,128)S(1)}, f32[12,2,8,128]{3,2,1,0:T(8,128)S(1)}, f32[12,2,8,128]{3,2,1,0:...) custom-call(s32[1]{0:T(128)} %get-tuple-element.175.me_ref, ...), custom_call_target="tpu_custom_call" | custom-call | tf_op jit(solution)/shard_map/cond/branch_3_fun/pallas_call | solution.py:415
  77.0 2.9 %collective-permute-start.46 = (f32[12,2,8,128]{3,2,1,0:T(8,128)S(1)}, f32[12,2,8,128]{3,2,1,0:T(8,128)S(1)}, u32[]{:S(2)}, u32[]{:S(2)}) collective-permute-start(f32[12,2,8,128]{3,2,1,0:T(8,128)S(1)} %get-tuple-element.182), channel_id=1, source_target_pairs={{0,9},{1,8},{2,11},{3,10},{4,13},{5,12},{6,15},{7,14},{8,1},{9,0},... | collective-permute-start | bytes 294920 | tf_op jit(solution)/shard_map/cond/branch_3_fun/ppermute | solution.py:335
  80.7 2.5 %collective-permute-start.48 = (f32[12,2,8,128]{3,2,1,0:T(8,128)S(1)}, f32[12,2,8,128]{3,2,1,0:T(8,128)S(1)}, u32[]{:S(2)}, u32[]{:S(2)}) collective-permute-start(f32[12,2,8,128]{3,2,1,0:T(8,128)S(1)} %get-tuple-element.184), channel_id=1, source_target_pairs={{0,11},{1,10},{2,9},{3,8},{4,15},{5,14},{6,13},{7,12},{8,3},{9,2},... | collective-permute-start | bytes 294920 | tf_op jit(solution)/shard_map/cond/branch_3_fun/ppermute | solution.py:335
  83.6 7.9 %collective-permute-start.50 = (f32[12,2,8,128]{3,2,1,0:T(8,128)S(1)}, f32[12,2,8,128]{3,2,1,0:T(8,128)S(1)}, u32[]{:S(2)}, u32[]{:S(2)}) collective-permute-start(f32[12,2,8,128]{3,2,1,0:T(8,128)S(1)} %get-tuple-element.186), channel_id=1, source_target_pairs={{0,13},{1,12},{2,15},{3,14},{4,9},{5,8},{6,11},{7,10},{8,5},{9,4},... | collective-permute-start | bytes 294920 | tf_op jit(solution)/shard_map/cond/branch_3_fun/ppermute | solution.py:335
  91.7 1.8 %collective-permute-start.51 = (f32[12,2,8,128]{3,2,1,0:T(8,128)S(1)}, f32[12,2,8,128]{3,2,1,0:T(8,128)S(1)}, u32[]{:S(2)}, u32[]{:S(2)}) collective-permute-start(f32[12,2,8,128]{3,2,1,0:T(8,128)S(1)} %get-tuple-element.187), channel_id=1, source_target_pairs={{0,14},{1,15},{2,12},{3,13},{4,10},{5,11},{6,8},{7,9},{8,6},{9,7},... | collective-permute-start | bytes 294920 | tf_op jit(solution)/shard_map/cond/branch_3_fun/ppermute | solution.py:335
  93.8 4.2 %collective-permute-start.52 = (f32[12,2,8,128]{3,2,1,0:T(8,128)S(1)}, f32[12,2,8,128]{3,2,1,0:T(8,128)S(1)}, u32[]{:S(2)}, u32[]{:S(2)}) collective-permute-start(f32[12,2,8,128]{3,2,1,0:T(8,128)S(1)} %get-tuple-element.188), channel_id=1, source_target_pairs={{0,15},{1,14},{2,13},{3,12},{4,11},{5,10},{6,9},{7,8},{8,7},{9,6},... | collective-permute-start | bytes 294920 | tf_op jit(solution)/shard_map/cond/branch_3_fun/ppermute | solution.py:335
  98.0 5.8 %collective-permute-start.53 = (f32[12,2,8,128]{3,2,1,0:T(8,128)S(1)}, f32[12,2,8,128]{3,2,1,0:T(8,128)S(1)}, u32[]{:S(2)}, u32[]{:S(2)}) collective-permute-start(f32[12,2,8,128]{3,2,1,0:T(8,128)S(1)} %get-tuple-element.189), channel_id=1, source_target_pairs={{0,4},{1,5},{2,6},{3,7},{4,0},{5,1},{6,2},{7,3},{8,12},{9,13},{10,... | collective-permute-start | bytes 294920 | tf_op jit(solution)/shard_map/cond/branch_3_fun/ppermute | solution.py:335
  104.5 4.1 %collective-permute-done.50.refs_5_ = f32[12,2,8,128]{3,2,1,0:T(8,128)S(1)} collective-permute-done((f32[12,2,8,128]{3,2,1,0:T(8,128)S(1)}, f32[12,2,8,128]{3,2,1,0:T(8,128)S(1)}, u32[]{:S(2)}, u32[]{:S(2)}) %collective-permute-start.50) | collective-permute-done | bytes 98336 | tf_op jit(solution)/shard_map/cond/branch_3_fun/ppermute | solution.py:335
  108.7 2.3 %collective-permute-done.51.refs_6_ = f32[12,2,8,128]{3,2,1,0:T(8,128)S(1)} collective-permute-done((f32[12,2,8,128]{3,2,1,0:T(8,128)S(1)}, f32[12,2,8,128]{3,2,1,0:T(8,128)S(1)}, u32[]{:S(2)}, u32[]{:S(2)}) %collective-permute-start.51) | collective-permute-done | bytes 98336 | tf_op jit(solution)/shard_map/cond/branch_3_fun/ppermute | solution.py:335
  111.1 2.8 %collective-permute-done.52.refs_7_ = f32[12,2,8,128]{3,2,1,0:T(8,128)S(1)} collective-permute-done((f32[12,2,8,128]{3,2,1,0:T(8,128)S(1)}, f32[12,2,8,128]{3,2,1,0:T(8,128)S(1)}, u32[]{:S(2)}, u32[]{:S(2)}) %collective-permute-start.52) | collective-permute-done | bytes 98336 | tf_op jit(solution)/shard_map/cond/branch_3_fun/ppermute | solution.py:335
  114.7 1.5 %collective-permute-start.58 = (f32[12,2,8,128]{3,2,1,0:T(8,128)S(1)}, f32[12,2,8,128]{3,2,1,0:T(8,128)S(1)}, u32[]{:S(2)}, u32[]{:S(2)}) collective-permute-start(f32[12,2,8,128]{3,2,1,0:T(8,128)S(1)} %get-tuple-element.194), channel_id=1, source_target_pairs={{0,3},{1,2},{2,1},{3,0},{4,7},{5,6},{6,5},{7,4},{8,11},{9,10},{10,... | collective-permute-start | bytes 294920 | tf_op jit(solution)/shard_map/cond/branch_3_fun/ppermute | solution.py:335
  117.2 2.0 %collective-permute-done.57.refs_12_ = f32[12,2,8,128]{3,2,1,0:T(8,128)S(1)} collective-permute-done((f32[12,2,8,128]{3,2,1,0:T(8,128)S(1)}, f32[12,2,8,128]{3,2,1,0:T(8,128)S(1)}, u32[]{:S(2)}, u32[]{:S(2)}) %collective-permute-start.57) | collective-permute-done | bytes 98336 | tf_op jit(solution)/shard_map/cond/branch_3_fun/ppermute | solution.py:335
  119.2 2.1 %collective-permute-done.58.refs_13_ = f32[12,2,8,128]{3,2,1,0:T(8,128)S(1)} collective-permute-done((f32[12,2,8,128]{3,2,1,0:T(8,128)S(1)}, f32[12,2,8,128]{3,2,1,0:T(8,128)S(1)}, u32[]{:S(2)}, u32[]{:S(2)}) %collective-permute-start.58) | collective-permute-done | bytes 98336 | tf_op jit(solution)/shard_map/cond/branch_3_fun/ppermute | solution.py:335
  121.3 2.0 %branch_3_fun.3 = f32[2,1024,256]{2,1,0:T(8,128)} custom-call(s32[1]{0:T(128)} %get-tuple-element.175.me_ref, s32[16]{0:T(128)S(1)} %slice_bitcast_fusion.3.slot_ref, f32[16]{0:T(128)S(1)} %reshape.84.weight_ref, f32[12,2,8,128]{3,2,1,0:T(8,128)S(1)} %collective-permute-done.45.refs_0_, f32[12,2,8,128]{3,2,1,0:T(8,128)S(1)} %collective-permute-done.46.refs_1_, ...), custom_call_target="tpu_custom_call" | custom-call | tf_op jit(solution)/shard_map/cond/branch_3_fun/pallas_call | solution.py:420
  (67 shorter events, 17.5 us)
Async XLA Ops:
  0.0 9.1 %copy-start.5 = (s32[8,2]{0,1:T(2,128)S(1)}, s32[8,2]{0,1:T(2,128)}, u32[]{:S(2)}) copy-start(s32[8,2]{0,1:T(2,128)} %param.14) | copy-start | bytes 196
  2.6 71.3 %all-to-all-start = ((f32[16,8,8,128]{3,2,1,0:T(8,128)}), f32[16,8,8,128]{3,2,1,0:T(8,128)S(1)}, u32[]{:S(2)}, u32[]{:S(2)}) async-start(f32[16,8,8,128]{3,2,1,0:T(8,128)} %shard_map.69), calls=%async_computation | async-start | bytes 1048576 | tf_op jit(solution)/shard_map/all_to_all | solution.py:362
  12.8 21.0 %collective-permute-start.105 = (f32[25,8,128]{2,1,0:T(8,128)S(1)}, f32[25,8,128]{2,1,0:T(8,128)S(1)}, u32[]{:S(2)}, u32[]{:S(2)}) collective-permute-start(f32[25,8,128]{2,1,0:T(8,128)S(1)} %get-tuple-element.283), channel_id=1, source_target_pairs={{0,8},{1,9},{2,10},{3,11},{4,12},{5,13},{6,14},{7,15},{8,0},{9,1},... | collective-permute-start | bytes 307208 | tf_op jit(solution)/shard_map/ppermute | solution.py:335
  14.9 21.3 %collective-permute-start.106 = (f32[25,8,128]{2,1,0:T(8,128)S(1)}, f32[25,8,128]{2,1,0:T(8,128)S(1)}, u32[]{:S(2)}, u32[]{:S(2)}) collective-permute-start(f32[25,8,128]{2,1,0:T(8,128)S(1)} %get-tuple-element.284), channel_id=1, source_target_pairs={{0,9},{1,8},{2,11},{3,10},{4,13},{5,12},{6,15},{7,14},{8,1},{9,0},... | collective-permute-start | bytes 307208 | tf_op jit(solution)/shard_map/ppermute | solution.py:335
  15.8 22.4 %collective-permute-start.107 = (f32[25,8,128]{2,1,0:T(8,128)S(1)}, f32[25,8,128]{2,1,0:T(8,128)S(1)}, u32[]{:S(2)}, u32[]{:S(2)}) collective-permute-start(f32[25,8,128]{2,1,0:T(8,128)S(1)} %get-tuple-element.285), channel_id=1, source_target_pairs={{0,10},{1,11},{2,8},{3,9},{4,14},{5,15},{6,12},{7,13},{8,2},{9,3},... | collective-permute-start | bytes 307208 | tf_op jit(solution)/shard_map/ppermute | solution.py:335
  17.8 26.9 %collective-permute-start.108 = (f32[25,8,128]{2,1,0:T(8,128)S(1)}, f32[25,8,128]{2,1,0:T(8,128)S(1)}, u32[]{:S(2)}, u32[]{:S(2)}) collective-permute-start(f32[25,8,128]{2,1,0:T(8,128)S(1)} %get-tuple-element.286), channel_id=1, source_target_pairs={{0,11},{1,10},{2,9},{3,8},{4,15},{5,14},{6,13},{7,12},{8,3},{9,2},... | collective-permute-start | bytes 307208 | tf_op jit(solution)/shard_map/ppermute | solution.py:335
  19.0 30.8 %collective-permute-start.109 = (f32[25,8,128]{2,1,0:T(8,128)S(1)}, f32[25,8,128]{2,1,0:T(8,128)S(1)}, u32[]{:S(2)}, u32[]{:S(2)}) collective-permute-start(f32[25,8,128]{2,1,0:T(8,128)S(1)} %get-tuple-element.287), channel_id=1, source_target_pairs={{0,12},{1,13},{2,14},{3,15},{4,8},{5,9},{6,10},{7,11},{8,4},{9,5},... | collective-permute-start | bytes 307208 | tf_op jit(solution)/shard_map/ppermute | solution.py:335
  33.8 20.5 %collective-permute-start.110 = (f32[25,8,128]{2,1,0:T(8,128)S(1)}, f32[25,8,128]{2,1,0:T(8,128)S(1)}, u32[]{:S(2)}, u32[]{:S(2)}) collective-permute-start(f32[25,8,128]{2,1,0:T(8,128)S(1)} %get-tuple-element.288), channel_id=1, source_target_pairs={{0,13},{1,12},{2,15},{3,14},{4,9},{5,8},{6,11},{7,10},{8,5},{9,4},... | collective-permute-start | bytes 307208 | tf_op jit(solution)/shard_map/ppermute | solution.py:335
  36.2 19.1 %collective-permute-start.111 = (f32[25,8,128]{2,1,0:T(8,128)S(1)}, f32[25,8,128]{2,1,0:T(8,128)S(1)}, u32[]{:S(2)}, u32[]{:S(2)}) collective-permute-start(f32[25,8,128]{2,1,0:T(8,128)S(1)} %get-tuple-element.289), channel_id=1, source_target_pairs={{0,14},{1,15},{2,12},{3,13},{4,10},{5,11},{6,8},{7,9},{8,6},{9,7},... | collective-permute-start | bytes 307208 | tf_op jit(solution)/shard_map/ppermute | solution.py:335
  38.1 20.2 %collective-permute-start.112 = (f32[25,8,128]{2,1,0:T(8,128)S(1)}, f32[25,8,128]{2,1,0:T(8,128)S(1)}, u32[]{:S(2)}, u32[]{:S(2)}) collective-permute-start(f32[25,8,128]{2,1,0:T(8,128)S(1)} %get-tuple-element.290), channel_id=1, source_target_pairs={{0,15},{1,14},{2,13},{3,12},{4,11},{5,10},{6,9},{7,8},{8,7},{9,6},... | collective-permute-start | bytes 307208 | tf_op jit(solution)/shard_map/ppermute | solution.py:335
  44.7 15.6 %collective-permute-start.113 = (f32[25,8,128]{2,1,0:T(8,128)S(1)}, f32[25,8,128]{2,1,0:T(8,128)S(1)}, u32[]{:S(2)}, u32[]{:S(2)}) collective-permute-start(f32[25,8,128]{2,1,0:T(8,128)S(1)} %get-tuple-element.291), channel_id=1, source_target_pairs={{0,4},{1,5},{2,6},{3,7},{4,0},{5,1},{6,2},{7,3},{8,12},{9,13},{10,... | collective-permute-start | bytes 307208 | tf_op jit(solution)/shard_map/ppermute | solution.py:335
  49.8 10.6 %collective-permute-start.114 = (f32[25,8,128]{2,1,0:T(8,128)S(1)}, f32[25,8,128]{2,1,0:T(8,128)S(1)}, u32[]{:S(2)}, u32[]{:S(2)}) collective-permute-start(f32[25,8,128]{2,1,0:T(8,128)S(1)} %get-tuple-element.292), channel_id=1, source_target_pairs={{0,5},{1,4},{2,7},{3,6},{4,1},{5,0},{6,3},{7,2},{8,13},{9,12},{10,... | collective-permute-start | bytes 307208 | tf_op jit(solution)/shard_map/ppermute | solution.py:335
  54.3 6.5 %collective-permute-start.115 = (f32[25,8,128]{2,1,0:T(8,128)S(1)}, f32[25,8,128]{2,1,0:T(8,128)S(1)}, u32[]{:S(2)}, u32[]{:S(2)}) collective-permute-start(f32[25,8,128]{2,1,0:T(8,128)S(1)} %get-tuple-element.293), channel_id=1, source_target_pairs={{0,6},{1,7},{2,4},{3,5},{4,2},{5,3},{6,0},{7,1},{8,14},{9,15},{10,... | collective-permute-start | bytes 307208 | tf_op jit(solution)/shard_map/ppermute | solution.py:335
  55.3 6.7 %collective-permute-start.116 = (f32[25,8,128]{2,1,0:T(8,128)S(1)}, f32[25,8,128]{2,1,0:T(8,128)S(1)}, u32[]{:S(2)}, u32[]{:S(2)}) collective-permute-start(f32[25,8,128]{2,1,0:T(8,128)S(1)} %get-tuple-element.294), channel_id=1, source_target_pairs={{0,7},{1,6},{2,5},{3,4},{4,3},{5,2},{6,1},{7,0},{8,15},{9,14},{10,... | collective-permute-start | bytes 307208 | tf_op jit(solution)/shard_map/ppermute | solution.py:335
  58.4 6.2 %collective-permute-start.117 = (f32[25,8,128]{2,1,0:T(8,128)S(1)}, f32[25,8,128]{2,1,0:T(8,128)S(1)}, u32[]{:S(2)}, u32[]{:S(2)}) collective-permute-start(f32[25,8,128]{2,1,0:T(8,128)S(1)} %get-tuple-element.295), channel_id=1, source_target_pairs={{0,2},{1,3},{2,0},{3,1},{4,6},{5,7},{6,4},{7,5},{8,10},{9,11},{10,... | collective-permute-start | bytes 307208 | tf_op jit(solution)/shard_map/ppermute | solution.py:335
  60.4 6.5 %collective-permute-start.118 = (f32[25,8,128]{2,1,0:T(8,128)S(1)}, f32[25,8,128]{2,1,0:T(8,128)S(1)}, u32[]{:S(2)}, u32[]{:S(2)}) collective-permute-start(f32[25,8,128]{2,1,0:T(8,128)S(1)} %get-tuple-element.296), channel_id=1, source_target_pairs={{0,3},{1,2},{2,1},{3,0},{4,7},{5,6},{6,5},{7,4},{8,11},{9,10},{10,... | collective-permute-start | bytes 307208 | tf_op jit(solution)/shard_map/ppermute | solution.py:335
  60.4 6.5 %collective-permute-start.119 = (f32[25,8,128]{2,1,0:T(8,128)S(1)}, f32[25,8,128]{2,1,0:T(8,128)S(1)}, u32[]{:S(2)}, u32[]{:S(2)}) collective-permute-start(f32[25,8,128]{2,1,0:T(8,128)S(1)} %get-tuple-element.297), channel_id=1, source_target_pairs={{0,1},{1,0},{2,3},{3,2},{4,5},{5,4},{6,7},{7,6},{8,9},{9,8},{10,11... | collective-permute-start | bytes 307208 | tf_op jit(solution)/shard_map/ppermute | solution.py:335
  77.0 6.6 %collective-permute-start.45 = (f32[12,2,8,128]{3,2,1,0:T(8,128)S(1)}, f32[12,2,8,128]{3,2,1,0:T(8,128)S(1)}, u32[]{:S(2)}, u32[]{:S(2)}) collective-permute-start(f32[12,2,8,128]{3,2,1,0:T(8,128)S(1)} %get-tuple-element.181), channel_id=1, source_target_pairs={{0,8},{1,9},{2,10},{3,11},{4,12},{5,13},{6,14},{7,15},{8,0},{9,1},... | collective-permute-start | bytes 294920 | tf_op jit(solution)/shard_map/cond/branch_3_fun/ppermute | solution.py:335
  77.0 14.6 %collective-permute-start.46 = (f32[12,2,8,128]{3,2,1,0:T(8,128)S(1)}, f32[12,2,8,128]{3,2,1,0:T(8,128)S(1)}, u32[]{:S(2)}, u32[]{:S(2)}) collective-permute-start(f32[12,2,8,128]{3,2,1,0:T(8,128)S(1)} %get-tuple-element.182), channel_id=1, source_target_pairs={{0,9},{1,8},{2,11},{3,10},{4,13},{5,12},{6,15},{7,14},{8,1},{9,0},... | collective-permute-start | bytes 294920 | tf_op jit(solution)/shard_map/cond/branch_3_fun/ppermute | solution.py:335
  80.0 13.8 %collective-permute-start.47 = (f32[12,2,8,128]{3,2,1,0:T(8,128)S(1)}, f32[12,2,8,128]{3,2,1,0:T(8,128)S(1)}, u32[]{:S(2)}, u32[]{:S(2)}) collective-permute-start(f32[12,2,8,128]{3,2,1,0:T(8,128)S(1)} %get-tuple-element.183), channel_id=1, source_target_pairs={{0,10},{1,11},{2,8},{3,9},{4,14},{5,15},{6,12},{7,13},{8,2},{9,3},... | collective-permute-start | bytes 294920 | tf_op jit(solution)/shard_map/cond/branch_3_fun/ppermute | solution.py:335
  80.7 17.3 %collective-permute-start.48 = (f32[12,2,8,128]{3,2,1,0:T(8,128)S(1)}, f32[12,2,8,128]{3,2,1,0:T(8,128)S(1)}, u32[]{:S(2)}, u32[]{:S(2)}) collective-permute-start(f32[12,2,8,128]{3,2,1,0:T(8,128)S(1)} %get-tuple-element.184), channel_id=1, source_target_pairs={{0,11},{1,10},{2,9},{3,8},{4,15},{5,14},{6,13},{7,12},{8,3},{9,2},... | collective-permute-start | bytes 294920 | tf_op jit(solution)/shard_map/cond/branch_3_fun/ppermute | solution.py:335
  83.2 21.0 %collective-permute-start.49 = (f32[12,2,8,128]{3,2,1,0:T(8,128)S(1)}, f32[12,2,8,128]{3,2,1,0:T(8,128)S(1)}, u32[]{:S(2)}, u32[]{:S(2)}) collective-permute-start(f32[12,2,8,128]{3,2,1,0:T(8,128)S(1)} %get-tuple-element.185), channel_id=1, source_target_pairs={{0,12},{1,13},{2,14},{3,15},{4,8},{5,9},{6,10},{7,11},{8,4},{9,5},... | collective-permute-start | bytes 294920 | tf_op jit(solution)/shard_map/cond/branch_3_fun/ppermute | solution.py:335
  83.6 25.0 %collective-permute-start.50 = (f32[12,2,8,128]{3,2,1,0:T(8,128)S(1)}, f32[12,2,8,128]{3,2,1,0:T(8,128)S(1)}, u32[]{:S(2)}, u32[]{:S(2)}) collective-permute-start(f32[12,2,8,128]{3,2,1,0:T(8,128)S(1)} %get-tuple-element.186), channel_id=1, source_target_pairs={{0,13},{1,12},{2,15},{3,14},{4,9},{5,8},{6,11},{7,10},{8,5},{9,4},... | collective-permute-start | bytes 294920 | tf_op jit(solution)/shard_map/cond/branch_3_fun/ppermute | solution.py:335
  91.7 19.4 %collective-permute-start.51 = (f32[12,2,8,128]{3,2,1,0:T(8,128)S(1)}, f32[12,2,8,128]{3,2,1,0:T(8,128)S(1)}, u32[]{:S(2)}, u32[]{:S(2)}) collective-permute-start(f32[12,2,8,128]{3,2,1,0:T(8,128)S(1)} %get-tuple-element.187), channel_id=1, source_target_pairs={{0,14},{1,15},{2,12},{3,13},{4,10},{5,11},{6,8},{7,9},{8,6},{9,7},... | collective-permute-start | bytes 294920 | tf_op jit(solution)/shard_map/cond/branch_3_fun/ppermute | solution.py:335
  93.8 20.1 %collective-permute-start.52 = (f32[12,2,8,128]{3,2,1,0:T(8,128)S(1)}, f32[12,2,8,128]{3,2,1,0:T(8,128)S(1)}, u32[]{:S(2)}, u32[]{:S(2)}) collective-permute-start(f32[12,2,8,128]{3,2,1,0:T(8,128)S(1)} %get-tuple-element.188), channel_id=1, source_target_pairs={{0,15},{1,14},{2,13},{3,12},{4,11},{5,10},{6,9},{7,8},{8,7},{9,6},... | collective-permute-start | bytes 294920 | tf_op jit(solution)/shard_map/cond/branch_3_fun/ppermute | solution.py:335
  98.0 16.7 %collective-permute-start.53 = (f32[12,2,8,128]{3,2,1,0:T(8,128)S(1)}, f32[12,2,8,128]{3,2,1,0:T(8,128)S(1)}, u32[]{:S(2)}, u32[]{:S(2)}) collective-permute-start(f32[12,2,8,128]{3,2,1,0:T(8,128)S(1)} %get-tuple-element.189), channel_id=1, source_target_pairs={{0,4},{1,5},{2,6},{3,7},{4,0},{5,1},{6,2},{7,3},{8,12},{9,13},{10,... | collective-permute-start | bytes 294920 | tf_op jit(solution)/shard_map/cond/branch_3_fun/ppermute | solution.py:335
  104.2 12.0 %collective-permute-start.54 = (f32[12,2,8,128]{3,2,1,0:T(8,128)S(1)}, f32[12,2,8,128]{3,2,1,0:T(8,128)S(1)}, u32[]{:S(2)}, u32[]{:S(2)}) collective-permute-start(f32[12,2,8,128]{3,2,1,0:T(8,128)S(1)} %get-tuple-element.190), channel_id=1, source_target_pairs={{0,5},{1,4},{2,7},{3,6},{4,1},{5,0},{6,3},{7,2},{8,13},{9,12},{10,... | collective-permute-start | bytes 294920 | tf_op jit(solution)/shard_map/cond/branch_3_fun/ppermute | solution.py:335
  108.6 7.8 %collective-permute-start.55 = (f32[12,2,8,128]{3,2,1,0:T(8,128)S(1)}, f32[12,2,8,128]{3,2,1,0:T(8,128)S(1)}, u32[]{:S(2)}, u32[]{:S(2)}) collective-permute-start(f32[12,2,8,128]{3,2,1,0:T(8,128)S(1)} %get-tuple-element.191), channel_id=1, source_target_pairs={{0,6},{1,7},{2,4},{3,5},{4,2},{5,3},{6,0},{7,1},{8,14},{9,15},{10,... | collective-permute-start | bytes 294920 | tf_op jit(solution)/shard_map/cond/branch_3_fun/ppermute | solution.py:335
  111.1 6.1 %collective-permute-start.56 = (f32[12,2,8,128]{3,2,1,0:T(8,128)S(1)}, f32[12,2,8,128]{3,2,1,0:T(8,128)S(1)}, u32[]{:S(2)}, u32[]{:S(2)}) collective-permute-start(f32[12,2,8,128]{3,2,1,0:T(8,128)S(1)} %get-tuple-element.192), channel_id=1, source_target_pairs={{0,7},{1,6},{2,5},{3,4},{4,3},{5,2},{6,1},{7,0},{8,15},{9,14},{10,... | collective-permute-start | bytes 294920 | tf_op jit(solution)/shard_map/cond/branch_3_fun/ppermute | solution.py:335
  113.8 5.3 %collective-permute-start.57 = (f32[12,2,8,128]{3,2,1,0:T(8,128)S(1)}, f32[12,2,8,128]{3,2,1,0:T(8,128)S(1)}, u32[]{:S(2)}, u32[]{:S(2)}) collective-permute-start(f32[12,2,8,128]{3,2,1,0:T(8,128)S(1)} %get-tuple-element.193), channel_id=1, source_target_pairs={{0,2},{1,3},{2,0},{3,1},{4,6},{5,7},{6,4},{7,5},{8,10},{9,11},{10,... | collective-permute-start | bytes 294920 | tf_op jit(solution)/shard_map/cond/branch_3_fun/ppermute | solution.py:335
  114.7 6.6 %collective-permute-start.58 = (f32[12,2,8,128]{3,2,1,0:T(8,128)S(1)}, f32[12,2,8,128]{3,2,1,0:T(8,128)S(1)}, u32[]{:S(2)}, u32[]{:S(2)}) collective-permute-start(f32[12,2,8,128]{3,2,1,0:T(8,128)S(1)} %get-tuple-element.194), channel_id=1, source_target_pairs={{0,3},{1,2},{2,1},{3,0},{4,7},{5,6},{6,5},{7,4},{8,11},{9,10},{10,... | collective-permute-start | bytes 294920 | tf_op jit(solution)/shard_map/cond/branch_3_fun/ppermute | solution.py:335
  116.2 5.1 %collective-permute-start.59 = (f32[12,2,8,128]{3,2,1,0:T(8,128)S(1)}, f32[12,2,8,128]{3,2,1,0:T(8,128)S(1)}, u32[]{:S(2)}, u32[]{:S(2)}) collective-permute-start(f32[12,2,8,128]{3,2,1,0:T(8,128)S(1)} %get-tuple-element.195), channel_id=1, source_target_pairs={{0,1},{1,0},{2,3},{3,2},{4,5},{5,4},{6,7},{7,6},{8,9},{9,8},{10,11... | collective-permute-start | bytes 294920 | tf_op jit(solution)/shard_map/cond/branch_3_fun/ppermute | solution.py:335
  (5 other events, 14.6 us)
where the time goes:
time: 125 us; the launch traced here: 123 us
  starting transfers between devices  55.7 us (45%)
  waiting for transfers between devices  46.4 us (37%)
  Pallas kernels  15.6 us (12%)
  other arithmetic  2.63 us (2%)
  local copies, waits for them, and re-layouts  2.05 us (2%)
    ppermute x30, starting transfers between devices, trade(): traded.append(lax.ppermute(value, 'col', pairs) if hop else value)  49.1 us
    ppermute x30, waiting for transfers between devices, trade(): traded.append(lax.ppermute(value, 'col', pairs) if hop else value)  46.4 us
    pallas_call x2, Pallas kernels, transform(): call(functools.partial(transform_kernel, devices, count, masks), outs, [V...  7.73 us
    all_to_all x1, starting transfers between devices, shards_tiled(): lax.all_to_all(message, 'col', split_axis=0, concat_axis=0, tiled=True)  6.53 us
    pallas_call x1, Pallas kernels, shards_tiled(): call(functools.partial(pack_each_kernel, 0, part), [shape(2 * early + 1,...  3.46 us
  transfers between devices with their start and end apart: 31, of which 19 were waited for; matrix products, arithmetic and copies ran while one was open for 2% of the time, Pallas kernels for 8%

commit v1 on v0

--- a/solution.py
+++ b/solution.py
@@ -91,32 +91,28 @@
 
 
 def pack_each_kernel(first, blocks, me_ref, slab_ref, mask_ref, *refs):
-    outs, (stage_ref, in_sem, out_sem) = refs[:-3], refs[-3:]
+    outs, sem = refs[:-1], refs[-1]
     halves = slab_ref.shape[4] // LANES
     me = me_ref[0]
-    gathers, puts = [], []
-    for number, hop in enumerate(travel_order(len(outs))):
+    copies = []
+    for hop, out in zip(travel_order(len(outs)), outs):
         for plane in range(2):
             for half in range(halves):
                 tile = (plane * halves + half) * blocks
                 lanes = slice(half * LANES, (half + 1) * LANES)
-                gathers.append(
+                copies.append(
                     pltpu.make_async_copy(
                         slab_ref.at[plane, first : first + blocks, me ^ hop, :, lanes],
-                        stage_ref.at[number, tile : tile + blocks],
-                        in_sem.at[len(gathers)],
+                        out.at[tile : tile + blocks],
+                        sem.at[len(copies)],
                     )
                 )
-    for copy in gathers:
+        copies.append(
+            pltpu.make_async_copy(mask_ref, out.at[2 * halves * blocks], sem.at[len(copies)])
+        )
+    for copy in copies:
         copy.start()
-    for number in range(len(outs)):
-        stage_ref[number, 2 * halves * blocks] = mask_ref[...]
-    for number, out in enumerate(outs):
-        for copy in gathers[number * 2 * halves : (number + 1) * 2 * halves]:
-            copy.wait()
-        puts.append(pltpu.make_async_copy(stage_ref.at[number], out, out_sem.at[number]))
-        puts[-1].start()
-    for copy in puts:
+    for copy in copies:
         copy.wait()
 
 
@@ -210,10 +206,11 @@
                         if dev & step:
                             continue
                         first, second = vals[dev], vals[dev | step]
-                        vals[dev] = jnp.where(odd_lane, pltpu.roll(second, step, 1), first)
-                        vals[dev | step] = jnp.where(
-                            odd_lane, second, pltpu.roll(first, LANES - step, 1)
+                        moved = jnp.take_along_axis(
+                            jnp.where(odd_lane, first, second), lane ^ step, axis=1
                         )
+                        vals[dev] = jnp.where(odd_lane, moved, first)
+                        vals[dev | step] = jnp.where(odd_lane, second, moved)
                 where = slice(plane * width + half * LANES, plane * width + (half + 1) * LANES)
                 for dev in range(devices):
                     high = vals[dev].astype(jnp.bfloat16)
@@ -344,19 +341,15 @@
     pieces = call(
         functools.partial(pack_each_kernel, 0, part),
         [shape(2 * early + 1, SUB, LANES)] * devices,
-        [SMEM_SPEC, HBM_SPEC, VMEM_SPEC],
-        [
-            pltpu.VMEM((devices, 2 * early + 1, SUB, LANES), jnp.float32),
-            pltpu.SemaphoreType.DMA((devices * 2 * halves,)),
-            pltpu.SemaphoreType.DMA((devices,)),
-        ],
+        [SMEM_SPEC, VMEM_SPEC, VMEM_SPEC],
+        [pltpu.SemaphoreType.DMA((devices * (2 * halves + 1),))],
         out_spec=PIECE_SPEC,
     )(me, dealt, flags)
     arrived = trade(pieces)
     message = call(
         functools.partial(pack_all_kernel, part, blocks - part),
         shape(devices, 2 * (tiles - early), SUB, LANES),
-        [HBM_SPEC],
+        [VMEM_SPEC],
         [pltpu.SemaphoreType.DMA((2 * (tiles - early),))],
     )(dealt)
     received = lax.all_to_all(message, "col", split_axis=0, concat_axis=0, tiled=True)

time: 125 us -> 123 us (0.984)
  Pallas kernels: 15.6 us -> 12.5 us
  waiting for transfers between devices: 46.4 us -> 48.4 us
    pallas_call x1, Pallas kernels: 3.46 us -> 1.43 us  [shards_tiled(): call(functools.partial(pack_each_kernel, 0, part), [shape(2 * early + 1,...]
    ppermute x30, waiting for transfers between devices: 46.4 us -> 48.4 us  [trade(): traded.append(lax.ppermute(value, 'col', pairs) if hop else value)]
  transfers between devices with their start and end apart: 31 -> 31, of which waited for: 19 -> 19; matrix products, arithmetic and copies ran while one was open for 2% -> 2% of each run, Pallas kernels for 8% -> 6%
where the time goes in v1:
time: 123 us; the launch traced here: 122 us
  starting transfers between devices  55.7 us (45%)
  waiting for transfers between devices  48.4 us (39%)
  Pallas kernels  12.5 us (10%)
  other arithmetic  2.63 us (2%)
  local copies, waits for them, and re-layouts  2.16 us (2%)
    ppermute x30, starting transfers between devices, trade(): traded.append(lax.ppermute(value, 'col', pairs) if hop else value)  49.2 us
    ppermute x30, waiting for transfers between devices, trade(): traded.append(lax.ppermute(value, 'col', pairs) if hop else value)  48.4 us
    pallas_call x2, Pallas kernels, transform(): call(functools.partial(transform_kernel, devices, count, masks), outs, [V...  6.64 us
    all_to_all x1, starting transfers between devices, shards_tiled(): lax.all_to_all(message, 'col', split_axis=0, concat_axis=0, tiled=True)  6.53 us
  transfers between devices with their start and end apart: 31, of which 19 were waited for; matrix products, arithmetic and copies ran while one was open for 2% of the time, Pallas kernels for 6%

profile of v1, /device:TPU:13, one launch (start us, length us, event | category | flops | bytes accessed | tf_op | source)
XLA Modules:
  0.0 122.4 jit_solution(480602505440386769)
XLA Ops:
  0.0 1.6 %copy-done = f32[2,1024,256]{2,1,0:T(8,128)S(1)} copy-done((f32[2,1024,256]{2,1,0:T(8,128)S(1)}, f32[2,1024,256]{2,1,0:T(8,128)}, u32[]{:S(2)}) %copy-start) | copy-done | bytes 2097176
  2.6 6.5 %all-to-all-start = ((f32[16,8,8,128]{3,2,1,0:T(8,128)}), f32[16,8,8,128]{3,2,1,0:T(8,128)S(1)}, u32[]{:S(2)}, u32[]{:S(2)}) async-start(f32[16,8,8,128]{3,2,1,0:T(8,128)} %shard_map.69), calls=%async_computation | async-start | bytes 1048576 | tf_op jit(solution)/shard_map/all_to_all | solution.py:355
  9.3 1.4 %shard_map.67 = (f32[25,8,128]{2,1,0:T(8,128)S(1)}, f32[25,8,128]{2,1,0:T(8,128)S(1)}, f32[25,8,128]{2,1,0:T(8,128)S(1)}, f32[25,8,128]{2,1,0:T(8,128)S(1)}, f32...) custom-call(s32[1]{0:T(128)} %bitcast.7.me_ref, ...), custom_call_target="tpu_custom_call" | custom-call | tf_op jit(solution)/shard_map/pallas_call | solution.py:341
  10.7 2.2 %collective-permute-start.105 = (f32[25,8,128]{2,1,0:T(8,128)S(1)}, f32[25,8,128]{2,1,0:T(8,128)S(1)}, u32[]{:S(2)}, u32[]{:S(2)}) collective-permute-start(f32[25,8,128]{2,1,0:T(8,128)S(1)} %get-tuple-element.283), channel_id=1, source_target_pairs={{0,8},{1,9},{2,10},{3,11},{4,12},{5,13},{6,14},{7,15},{8,0},{9,1},... | collective-permute-start | bytes 307208 | tf_op jit(solution)/shard_map/ppermute | solution.py:332
  13.7 2.1 %collective-permute-start.107 = (f32[25,8,128]{2,1,0:T(8,128)S(1)}, f32[25,8,128]{2,1,0:T(8,128)S(1)}, u32[]{:S(2)}, u32[]{:S(2)}) collective-permute-start(f32[25,8,128]{2,1,0:T(8,128)S(1)} %get-tuple-element.285), channel_id=1, source_target_pairs={{0,10},{1,11},{2,8},{3,9},{4,14},{5,15},{6,12},{7,13},{8,2},{9,3},... | collective-permute-start | bytes 307208 | tf_op jit(solution)/shard_map/ppermute | solution.py:332
  20.6 13.1 %collective-permute-done.105.refs_0_ = f32[25,8,128]{2,1,0:T(8,128)S(1)} collective-permute-done((f32[25,8,128]{2,1,0:T(8,128)S(1)}, f32[25,8,128]{2,1,0:T(8,128)S(1)}, u32[]{:S(2)}, u32[]{:S(2)}) %collective-permute-start.105) | collective-permute-done | bytes 102432 | tf_op jit(solution)/shard_map/ppermute | solution.py:332
  33.8 2.5 %collective-permute-start.110 = (f32[25,8,128]{2,1,0:T(8,128)S(1)}, f32[25,8,128]{2,1,0:T(8,128)S(1)}, u32[]{:S(2)}, u32[]{:S(2)}) collective-permute-start(f32[25,8,128]{2,1,0:T(8,128)S(1)} %get-tuple-element.288), channel_id=1, source_target_pairs={{0,13},{1,12},{2,15},{3,14},{4,9},{5,8},{6,11},{7,10},{8,5},{9,4},... | collective-permute-start | bytes 307208 | tf_op jit(solution)/shard_map/ppermute | solution.py:332
  38.1 2.4 %collective-permute-start.112 = (f32[25,8,128]{2,1,0:T(8,128)S(1)}, f32[25,8,128]{2,1,0:T(8,128)S(1)}, u32[]{:S(2)}, u32[]{:S(2)}) collective-permute-start(f32[25,8,128]{2,1,0:T(8,128)S(1)} %get-tuple-element.290), channel_id=1, source_target_pairs={{0,15},{1,14},{2,13},{3,12},{4,11},{5,10},{6,9},{7,8},{8,7},{9,6},... | collective-permute-start | bytes 307208 | tf_op jit(solution)/shard_map/ppermute | solution.py:332
  40.5 4.2 %collective-permute-done.108.refs_3_ = f32[25,8,128]{2,1,0:T(8,128)S(1)} collective-permute-done((f32[25,8,128]{2,1,0:T(8,128)S(1)}, f32[25,8,128]{2,1,0:T(8,128)S(1)}, u32[]{:S(2)}, u32[]{:S(2)}) %collective-permute-start.108) | collective-permute-done | bytes 102432 | tf_op jit(solution)/shard_map/ppermute | solution.py:332
  44.7 4.2 %collective-permute-start.113 = (f32[25,8,128]{2,1,0:T(8,128)S(1)}, f32[25,8,128]{2,1,0:T(8,128)S(1)}, u32[]{:S(2)}, u32[]{:S(2)}) collective-permute-start(f32[25,8,128]{2,1,0:T(8,128)S(1)} %get-tuple-element.291), channel_id=1, source_target_pairs={{0,4},{1,5},{2,6},{3,7},{4,0},{5,1},{6,2},{7,3},{8,12},{9,13},{10,... | collective-permute-start | bytes 307208 | tf_op jit(solution)/shard_map/ppermute | solution.py:332
  49.9 4.3 %collective-permute-done.110.refs_5_ = f32[25,8,128]{2,1,0:T(8,128)S(1)} collective-permute-done((f32[25,8,128]{2,1,0:T(8,128)S(1)}, f32[25,8,128]{2,1,0:T(8,128)S(1)}, u32[]{:S(2)}, u32[]{:S(2)}) %collective-permute-start.110) | collective-permute-done | bytes 102432 | tf_op jit(solution)/shard_map/ppermute | solution.py:332
  55.9 2.4 %collective-permute-done.112.refs_7_ = f32[25,8,128]{2,1,0:T(8,128)S(1)} collective-permute-done((f32[25,8,128]{2,1,0:T(8,128)S(1)}, f32[25,8,128]{2,1,0:T(8,128)S(1)}, u32[]{:S(2)}, u32[]{:S(2)}) %collective-permute-start.112) | collective-permute-done | bytes 102432 | tf_op jit(solution)/shard_map/ppermute | solution.py:332
  58.4 2.0 %collective-permute-start.117 = (f32[25,8,128]{2,1,0:T(8,128)S(1)}, f32[25,8,128]{2,1,0:T(8,128)S(1)}, u32[]{:S(2)}, u32[]{:S(2)}) collective-permute-start(f32[25,8,128]{2,1,0:T(8,128)S(1)} %get-tuple-element.295), channel_id=1, source_target_pairs={{0,2},{1,3},{2,0},{3,1},{4,6},{5,7},{6,4},{7,5},{8,10},{9,11},{10,... | collective-permute-start | bytes 307208 | tf_op jit(solution)/shard_map/ppermute | solution.py:332
  60.8 1.2 %collective-permute-done.116.refs_11_ = f32[25,8,128]{2,1,0:T(8,128)S(1)} collective-permute-done((f32[25,8,128]{2,1,0:T(8,128)S(1)}, f32[25,8,128]{2,1,0:T(8,128)S(1)}, u32[]{:S(2)}, u32[]{:S(2)}) %collective-permute-start.116) | collective-permute-done | bytes 102432 | tf_op jit(solution)/shard_map/ppermute | solution.py:332
  62.0 2.6 %collective-permute-done.117.refs_12_ = f32[25,8,128]{2,1,0:T(8,128)S(1)} collective-permute-done((f32[25,8,128]{2,1,0:T(8,128)S(1)}, f32[25,8,128]{2,1,0:T(8,128)S(1)}, u32[]{:S(2)}, u32[]{:S(2)}) %collective-permute-start.117) | collective-permute-done | bytes 102432 | tf_op jit(solution)/shard_map/ppermute | solution.py:332
  64.6 2.2 %collective-permute-done.118.refs_13_ = f32[25,8,128]{2,1,0:T(8,128)S(1)} collective-permute-done((f32[25,8,128]{2,1,0:T(8,128)S(1)}, f32[25,8,128]{2,1,0:T(8,128)S(1)}, u32[]{:S(2)}, u32[]{:S(2)}) %collective-permute-start.118) | collective-permute-done | bytes 102432 | tf_op jit(solution)/shard_map/ppermute | solution.py:332
  66.8 5.5 %shard_map.68 = (f32[16,12,2,8,128]{4,3,2,1,0:T(8,128)}, s32[16,128]{1,0:T(8,128)S(1)}, s32[16,128]{1,0:T(8,128)S(1)}, s32[1]{0:T(128)}) custom-call(f32[512,512]{1,0:T(8,128)S(1)} %maximum_maximum_fusion.table_ref, f32[16,512]{1,0:T(8,128)S(1)} %pad_maximum_fusion.twiddle_ref, f32[25,8,128]{2,1,0:T(8,128)S(1)} %collective-permute-done.105.refs_0_, ...), custom_call_target="tpu_custom_call" | custom-call | flops 1207959552 | bytes 16777216 | tf_op jit(solution)/shard_map/pallas_call | solution.py:384
  74.3 47.9 %conditional.1 = (f32[2,1024,256]{2,1,0:T(8,128)}) conditional(s32[]{:T(128)} %bitcast.9, (s32[1]{0:T(128)}, s32[16,128]{1,0:T(8,128)S(1)}, f32[16,12,2,8,128]{4,3,2,1,0:T(8,128)S(1)}, f32[16,4,2,8,128]{4,3,2,1,0:T(8,128)S(1)}, s32[16,128]{1,0:T(8,128)S(1)}, /*index=5*/f32[8,2]{0,1:T(2,128)S(1)}, (), ...), branch_computations={%region_1.2_spmd, %region_2.3_spmd, %region_3.4_spmd, %region_4.5_... | conditional | flops 208 | bytes 7865912 | solution.py:441
  74.4 1.5 %branch_3_fun.2 = (f32[12,2,8,128]{3,2,1,0:T(8,128)S(1)}, f32[12,2,8,128]{3,2,1,0:T(8,128)S(1)}, f32[12,2,8,128]{3,2,1,0:T(8,128)S(1)}, f32[12,2,8,128]{3,2,1,0:...) custom-call(s32[1]{0:T(128)} %get-tuple-element.175.me_ref, ...), custom_call_target="tpu_custom_call" | custom-call | tf_op jit(solution)/shard_map/cond/branch_3_fun/pallas_call | solution.py:408
  76.0 2.9 %collective-permute-start.46 = (f32[12,2,8,128]{3,2,1,0:T(8,128)S(1)}, f32[12,2,8,128]{3,2,1,0:T(8,128)S(1)}, u32[]{:S(2)}, u32[]{:S(2)}) collective-permute-start(f32[12,2,8,128]{3,2,1,0:T(8,128)S(1)} %get-tuple-element.182), channel_id=1, source_target_pairs={{0,9},{1,8},{2,11},{3,10},{4,13},{5,12},{6,15},{7,14},{8,1},{9,0},... | collective-permute-start | bytes 294920 | tf_op jit(solution)/shard_map/cond/branch_3_fun/ppermute | solution.py:332
  79.6 2.5 %collective-permute-start.48 = (f32[12,2,8,128]{3,2,1,0:T(8,128)S(1)}, f32[12,2,8,128]{3,2,1,0:T(8,128)S(1)}, u32[]{:S(2)}, u32[]{:S(2)}) collective-permute-start(f32[12,2,8,128]{3,2,1,0:T(8,128)S(1)} %get-tuple-element.184), channel_id=1, source_target_pairs={{0,11},{1,10},{2,9},{3,8},{4,15},{5,14},{6,13},{7,12},{8,3},{9,2},... | collective-permute-start | bytes 294920 | tf_op jit(solution)/shard_map/cond/branch_3_fun/ppermute | solution.py:332
  82.5 7.9 %collective-permute-start.50 = (f32[12,2,8,128]{3,2,1,0:T(8,128)S(1)}, f32[12,2,8,128]{3,2,1,0:T(8,128)S(1)}, u32[]{:S(2)}, u32[]{:S(2)}) collective-permute-start(f32[12,2,8,128]{3,2,1,0:T(8,128)S(1)} %get-tuple-element.186), channel_id=1, source_target_pairs={{0,13},{1,12},{2,15},{3,14},{4,9},{5,8},{6,11},{7,10},{8,5},{9,4},... | collective-permute-start | bytes 294920 | tf_op jit(solution)/shard_map/cond/branch_3_fun/ppermute | solution.py:332
  90.6 1.8 %collective-permute-start.51 = (f32[12,2,8,128]{3,2,1,0:T(8,128)S(1)}, f32[12,2,8,128]{3,2,1,0:T(8,128)S(1)}, u32[]{:S(2)}, u32[]{:S(2)}) collective-permute-start(f32[12,2,8,128]{3,2,1,0:T(8,128)S(1)} %get-tuple-element.187), channel_id=1, source_target_pairs={{0,14},{1,15},{2,12},{3,13},{4,10},{5,11},{6,8},{7,9},{8,6},{9,7},... | collective-permute-start | bytes 294920 | tf_op jit(solution)/shard_map/cond/branch_3_fun/ppermute | solution.py:332
  92.7 4.2 %collective-permute-start.52 = (f32[12,2,8,128]{3,2,1,0:T(8,128)S(1)}, f32[12,2,8,128]{3,2,1,0:T(8,128)S(1)}, u32[]{:S(2)}, u32[]{:S(2)}) collective-permute-start(f32[12,2,8,128]{3,2,1,0:T(8,128)S(1)} %get-tuple-element.188), channel_id=1, source_target_pairs={{0,15},{1,14},{2,13},{3,12},{4,11},{5,10},{6,9},{7,8},{8,7},{9,6},... | collective-permute-start | bytes 294920 | tf_op jit(solution)/shard_map/cond/branch_3_fun/ppermute | solution.py:332
  96.9 5.8 %collective-permute-start.53 = (f32[12,2,8,128]{3,2,1,0:T(8,128)S(1)}, f32[12,2,8,128]{3,2,1,0:T(8,128)S(1)}, u32[]{:S(2)}, u32[]{:S(2)}) collective-permute-start(f32[12,2,8,128]{3,2,1,0:T(8,128)S(1)} %get-tuple-element.189), channel_id=1, source_target_pairs={{0,4},{1,5},{2,6},{3,7},{4,0},{5,1},{6,2},{7,3},{8,12},{9,13},{10,... | collective-permute-start | bytes 294920 | tf_op jit(solution)/shard_map/cond/branch_3_fun/ppermute | solution.py:332
  103.4 4.1 %collective-permute-done.50.refs_5_ = f32[12,2,8,128]{3,2,1,0:T(8,128)S(1)} collective-permute-done((f32[12,2,8,128]{3,2,1,0:T(8,128)S(1)}, f32[12,2,8,128]{3,2,1,0:T(8,128)S(1)}, u32[]{:S(2)}, u32[]{:S(2)}) %collective-permute-start.50) | collective-permute-done | bytes 98336 | tf_op jit(solution)/shard_map/cond/branch_3_fun/ppermute | solution.py:332
  107.7 2.3 %collective-permute-done.51.refs_6_ = f32[12,2,8,128]{3,2,1,0:T(8,128)S(1)} collective-permute-done((f32[12,2,8,128]{3,2,1,0:T(8,128)S(1)}, f32[12,2,8,128]{3,2,1,0:T(8,128)S(1)}, u32[]{:S(2)}, u32[]{:S(2)}) %collective-permute-start.51) | collective-permute-done | bytes 98336 | tf_op jit(solution)/shard_map/cond/branch_3_fun/ppermute | solution.py:332
  110.0 2.8 %collective-permute-done.52.refs_7_ = f32[12,2,8,128]{3,2,1,0:T(8,128)S(1)} collective-permute-done((f32[12,2,8,128]{3,2,1,0:T(8,128)S(1)}, f32[12,2,8,128]{3,2,1,0:T(8,128)S(1)}, u32[]{:S(2)}, u32[]{:S(2)}) %collective-permute-start.52) | collective-permute-done | bytes 98336 | tf_op jit(solution)/shard_map/cond/branch_3_fun/ppermute | solution.py:332
  113.6 1.5 %collective-permute-start.58 = (f32[12,2,8,128]{3,2,1,0:T(8,128)S(1)}, f32[12,2,8,128]{3,2,1,0:T(8,128)S(1)}, u32[]{:S(2)}, u32[]{:S(2)}) collective-permute-start(f32[12,2,8,128]{3,2,1,0:T(8,128)S(1)} %get-tuple-element.194), channel_id=1, source_target_pairs={{0,3},{1,2},{2,1},{3,0},{4,7},{5,6},{6,5},{7,4},{8,11},{9,10},{10,... | collective-permute-start | bytes 294920 | tf_op jit(solution)/shard_map/cond/branch_3_fun/ppermute | solution.py:332
  116.1 2.0 %collective-permute-done.57.refs_12_ = f32[12,2,8,128]{3,2,1,0:T(8,128)S(1)} collective-permute-done((f32[12,2,8,128]{3,2,1,0:T(8,128)S(1)}, f32[12,2,8,128]{3,2,1,0:T(8,128)S(1)}, u32[]{:S(2)}, u32[]{:S(2)}) %collective-permute-start.57) | collective-permute-done | bytes 98336 | tf_op jit(solution)/shard_map/cond/branch_3_fun/ppermute | solution.py:332
  118.1 2.1 %collective-permute-done.58.refs_13_ = f32[12,2,8,128]{3,2,1,0:T(8,128)S(1)} collective-permute-done((f32[12,2,8,128]{3,2,1,0:T(8,128)S(1)}, f32[12,2,8,128]{3,2,1,0:T(8,128)S(1)}, u32[]{:S(2)}, u32[]{:S(2)}) %collective-permute-start.58) | collective-permute-done | bytes 98336 | tf_op jit(solution)/shard_map/cond/branch_3_fun/ppermute | solution.py:332
  120.2 2.0 %branch_3_fun.3 = f32[2,1024,256]{2,1,0:T(8,128)} custom-call(s32[1]{0:T(128)} %get-tuple-element.175.me_ref, s32[16]{0:T(128)S(1)} %slice_bitcast_fusion.3.slot_ref, f32[16]{0:T(128)S(1)} %reshape.84.weight_ref, f32[12,2,8,128]{3,2,1,0:T(8,128)S(1)} %collective-permute-done.45.refs_0_, f32[12,2,8,128]{3,2,1,0:T(8,128)S(1)} %collective-permute-done.46.refs_1_, ...), custom_call_target="tpu_custom_call" | custom-call | tf_op jit(solution)/shard_map/cond/branch_3_fun/pallas_call | solution.py:413
  (67 shorter events, 17.5 us)
Async XLA Ops:
  0.0 9.1 %copy-start.5 = (s32[8,2]{0,1:T(2,128)S(1)}, s32[8,2]{0,1:T(2,128)}, u32[]{:S(2)}) copy-start(s32[8,2]{0,1:T(2,128)} %param.14) | copy-start | bytes 196
  2.6 70.3 %all-to-all-start = ((f32[16,8,8,128]{3,2,1,0:T(8,128)}), f32[16,8,8,128]{3,2,1,0:T(8,128)S(1)}, u32[]{:S(2)}, u32[]{:S(2)}) async-start(f32[16,8,8,128]{3,2,1,0:T(8,128)} %shard_map.69), calls=%async_computation | async-start | bytes 1048576 | tf_op jit(solution)/shard_map/all_to_all | solution.py:355
  10.7 23.0 %collective-permute-start.105 = (f32[25,8,128]{2,1,0:T(8,128)S(1)}, f32[25,8,128]{2,1,0:T(8,128)S(1)}, u32[]{:S(2)}, u32[]{:S(2)}) collective-permute-start(f32[25,8,128]{2,1,0:T(8,128)S(1)} %get-tuple-element.283), channel_id=1, source_target_pairs={{0,8},{1,9},{2,10},{3,11},{4,12},{5,13},{6,14},{7,15},{8,0},{9,1},... | collective-permute-start | bytes 307208 | tf_op jit(solution)/shard_map/ppermute | solution.py:332
  12.9 23.4 %collective-permute-start.106 = (f32[25,8,128]{2,1,0:T(8,128)S(1)}, f32[25,8,128]{2,1,0:T(8,128)S(1)}, u32[]{:S(2)}, u32[]{:S(2)}) collective-permute-start(f32[25,8,128]{2,1,0:T(8,128)S(1)} %get-tuple-element.284), channel_id=1, source_target_pairs={{0,9},{1,8},{2,11},{3,10},{4,13},{5,12},{6,15},{7,14},{8,1},{9,0},... | collective-permute-start | bytes 307208 | tf_op jit(solution)/shard_map/ppermute | solution.py:332
  13.7 24.4 %collective-permute-start.107 = (f32[25,8,128]{2,1,0:T(8,128)S(1)}, f32[25,8,128]{2,1,0:T(8,128)S(1)}, u32[]{:S(2)}, u32[]{:S(2)}) collective-permute-start(f32[25,8,128]{2,1,0:T(8,128)S(1)} %get-tuple-element.285), channel_id=1, source_target_pairs={{0,10},{1,11},{2,8},{3,9},{4,14},{5,15},{6,12},{7,13},{8,2},{9,3},... | collective-permute-start | bytes 307208 | tf_op jit(solution)/shard_map/ppermute | solution.py:332
  15.8 28.9 %collective-permute-start.108 = (f32[25,8,128]{2,1,0:T(8,128)S(1)}, f32[25,8,128]{2,1,0:T(8,128)S(1)}, u32[]{:S(2)}, u32[]{:S(2)}) collective-permute-start(f32[25,8,128]{2,1,0:T(8,128)S(1)} %get-tuple-element.286), channel_id=1, source_target_pairs={{0,11},{1,10},{2,9},{3,8},{4,15},{5,14},{6,13},{7,12},{8,3},{9,2},... | collective-permute-start | bytes 307208 | tf_op jit(solution)/shard_map/ppermute | solution.py:332
  17.0 32.8 %collective-permute-start.109 = (f32[25,8,128]{2,1,0:T(8,128)S(1)}, f32[25,8,128]{2,1,0:T(8,128)S(1)}, u32[]{:S(2)}, u32[]{:S(2)}) collective-permute-start(f32[25,8,128]{2,1,0:T(8,128)S(1)} %get-tuple-element.287), channel_id=1, source_target_pairs={{0,12},{1,13},{2,14},{3,15},{4,8},{5,9},{6,10},{7,11},{8,4},{9,5},... | collective-permute-start | bytes 307208 | tf_op jit(solution)/shard_map/ppermute | solution.py:332
  33.8 20.5 %collective-permute-start.110 = (f32[25,8,128]{2,1,0:T(8,128)S(1)}, f32[25,8,128]{2,1,0:T(8,128)S(1)}, u32[]{:S(2)}, u32[]{:S(2)}) collective-permute-start(f32[25,8,128]{2,1,0:T(8,128)S(1)} %get-tuple-element.288), channel_id=1, source_target_pairs={{0,13},{1,12},{2,15},{3,14},{4,9},{5,8},{6,11},{7,10},{8,5},{9,4},... | collective-permute-start | bytes 307208 | tf_op jit(solution)/shard_map/ppermute | solution.py:332
  36.2 19.1 %collective-permute-start.111 = (f32[25,8,128]{2,1,0:T(8,128)S(1)}, f32[25,8,128]{2,1,0:T(8,128)S(1)}, u32[]{:S(2)}, u32[]{:S(2)}) collective-permute-start(f32[25,8,128]{2,1,0:T(8,128)S(1)} %get-tuple-element.289), channel_id=1, source_target_pairs={{0,14},{1,15},{2,12},{3,13},{4,10},{5,11},{6,8},{7,9},{8,6},{9,7},... | collective-permute-start | bytes 307208 | tf_op jit(solution)/shard_map/ppermute | solution.py:332
  38.1 20.2 %collective-permute-start.112 = (f32[25,8,128]{2,1,0:T(8,128)S(1)}, f32[25,8,128]{2,1,0:T(8,128)S(1)}, u32[]{:S(2)}, u32[]{:S(2)}) collective-permute-start(f32[25,8,128]{2,1,0:T(8,128)S(1)} %get-tuple-element.290), channel_id=1, source_target_pairs={{0,15},{1,14},{2,13},{3,12},{4,11},{5,10},{6,9},{7,8},{8,7},{9,6},... | collective-permute-start | bytes 307208 | tf_op jit(solution)/shard_map/ppermute | solution.py:332
  44.7 15.6 %collective-permute-start.113 = (f32[25,8,128]{2,1,0:T(8,128)S(1)}, f32[25,8,128]{2,1,0:T(8,128)S(1)}, u32[]{:S(2)}, u32[]{:S(2)}) collective-permute-start(f32[25,8,128]{2,1,0:T(8,128)S(1)} %get-tuple-element.291), channel_id=1, source_target_pairs={{0,4},{1,5},{2,6},{3,7},{4,0},{5,1},{6,2},{7,3},{8,12},{9,13},{10,... | collective-permute-start | bytes 307208 | tf_op jit(solution)/shard_map/ppermute | solution.py:332
  49.8 10.6 %collective-permute-start.114 = (f32[25,8,128]{2,1,0:T(8,128)S(1)}, f32[25,8,128]{2,1,0:T(8,128)S(1)}, u32[]{:S(2)}, u32[]{:S(2)}) collective-permute-start(f32[25,8,128]{2,1,0:T(8,128)S(1)} %get-tuple-element.292), channel_id=1, source_target_pairs={{0,5},{1,4},{2,7},{3,6},{4,1},{5,0},{6,3},{7,2},{8,13},{9,12},{10,... | collective-permute-start | bytes 307208 | tf_op jit(solution)/shard_map/ppermute | solution.py:332
  54.3 6.5 %collective-permute-start.115 = (f32[25,8,128]{2,1,0:T(8,128)S(1)}, f32[25,8,128]{2,1,0:T(8,128)S(1)}, u32[]{:S(2)}, u32[]{:S(2)}) collective-permute-start(f32[25,8,128]{2,1,0:T(8,128)S(1)} %get-tuple-element.293), channel_id=1, source_target_pairs={{0,6},{1,7},{2,4},{3,5},{4,2},{5,3},{6,0},{7,1},{8,14},{9,15},{10,... | collective-permute-start | bytes 307208 | tf_op jit(solution)/shard_map/ppermute | solution.py:332
  55.3 6.7 %collective-permute-start.116 = (f32[25,8,128]{2,1,0:T(8,128)S(1)}, f32[25,8,128]{2,1,0:T(8,128)S(1)}, u32[]{:S(2)}, u32[]{:S(2)}) collective-permute-start(f32[25,8,128]{2,1,0:T(8,128)S(1)} %get-tuple-element.294), channel_id=1, source_target_pairs={{0,7},{1,6},{2,5},{3,4},{4,3},{5,2},{6,1},{7,0},{8,15},{9,14},{10,... | collective-permute-start | bytes 307208 | tf_op jit(solution)/shard_map/ppermute | solution.py:332
  58.4 6.2 %collective-permute-start.117 = (f32[25,8,128]{2,1,0:T(8,128)S(1)}, f32[25,8,128]{2,1,0:T(8,128)S(1)}, u32[]{:S(2)}, u32[]{:S(2)}) collective-permute-start(f32[25,8,128]{2,1,0:T(8,128)S(1)} %get-tuple-element.295), channel_id=1, source_target_pairs={{0,2},{1,3},{2,0},{3,1},{4,6},{5,7},{6,4},{7,5},{8,10},{9,11},{10,... | collective-permute-start | bytes 307208 | tf_op jit(solution)/shard_map/ppermute | solution.py:332
  60.4 6.5 %collective-permute-start.118 = (f32[25,8,128]{2,1,0:T(8,128)S(1)}, f32[25,8,128]{2,1,0:T(8,128)S(1)}, u32[]{:S(2)}, u32[]{:S(2)}) collective-permute-start(f32[25,8,128]{2,1,0:T(8,128)S(1)} %get-tuple-element.296), channel_id=1, source_target_pairs={{0,3},{1,2},{2,1},{3,0},{4,7},{5,6},{6,5},{7,4},{8,11},{9,10},{10,... | collective-permute-start | bytes 307208 | tf_op jit(solution)/shard_map/ppermute | solution.py:332
  60.4 6.5 %collective-permute-start.119 = (f32[25,8,128]{2,1,0:T(8,128)S(1)}, f32[25,8,128]{2,1,0:T(8,128)S(1)}, u32[]{:S(2)}, u32[]{:S(2)}) collective-permute-start(f32[25,8,128]{2,1,0:T(8,128)S(1)} %get-tuple-element.297), channel_id=1, source_target_pairs={{0,1},{1,0},{2,3},{3,2},{4,5},{5,4},{6,7},{7,6},{8,9},{9,8},{10,11... | collective-permute-start | bytes 307208 | tf_op jit(solution)/shard_map/ppermute | solution.py:332
  75.9 6.6 %collective-permute-start.45 = (f32[12,2,8,128]{3,2,1,0:T(8,128)S(1)}, f32[12,2,8,128]{3,2,1,0:T(8,128)S(1)}, u32[]{:S(2)}, u32[]{:S(2)}) collective-permute-start(f32[12,2,8,128]{3,2,1,0:T(8,128)S(1)} %get-tuple-element.181), channel_id=1, source_target_pairs={{0,8},{1,9},{2,10},{3,11},{4,12},{5,13},{6,14},{7,15},{8,0},{9,1},... | collective-permute-start | bytes 294920 | tf_op jit(solution)/shard_map/cond/branch_3_fun/ppermute | solution.py:332
  76.0 14.6 %collective-permute-start.46 = (f32[12,2,8,128]{3,2,1,0:T(8,128)S(1)}, f32[12,2,8,128]{3,2,1,0:T(8,128)S(1)}, u32[]{:S(2)}, u32[]{:S(2)}) collective-permute-start(f32[12,2,8,128]{3,2,1,0:T(8,128)S(1)} %get-tuple-element.182), channel_id=1, source_target_pairs={{0,9},{1,8},{2,11},{3,10},{4,13},{5,12},{6,15},{7,14},{8,1},{9,0},... | collective-permute-start | bytes 294920 | tf_op jit(solution)/shard_map/cond/branch_3_fun/ppermute | solution.py:332
  78.9 13.8 %collective-permute-start.47 = (f32[12,2,8,128]{3,2,1,0:T(8,128)S(1)}, f32[12,2,8,128]{3,2,1,0:T(8,128)S(1)}, u32[]{:S(2)}, u32[]{:S(2)}) collective-permute-start(f32[12,2,8,128]{3,2,1,0:T(8,128)S(1)} %get-tuple-element.183), channel_id=1, source_target_pairs={{0,10},{1,11},{2,8},{3,9},{4,14},{5,15},{6,12},{7,13},{8,2},{9,3},... | collective-permute-start | bytes 294920 | tf_op jit(solution)/shard_map/cond/branch_3_fun/ppermute | solution.py:332
  79.6 17.3 %collective-permute-start.48 = (f32[12,2,8,128]{3,2,1,0:T(8,128)S(1)}, f32[12,2,8,128]{3,2,1,0:T(8,128)S(1)}, u32[]{:S(2)}, u32[]{:S(2)}) collective-permute-start(f32[12,2,8,128]{3,2,1,0:T(8,128)S(1)} %get-tuple-element.184), channel_id=1, source_target_pairs={{0,11},{1,10},{2,9},{3,8},{4,15},{5,14},{6,13},{7,12},{8,3},{9,2},... | collective-permute-start | bytes 294920 | tf_op jit(solution)/shard_map/cond/branch_3_fun/ppermute | solution.py:332
  82.1 21.0 %collective-permute-start.49 = (f32[12,2,8,128]{3,2,1,0:T(8,128)S(1)}, f32[12,2,8,128]{3,2,1,0:T(8,128)S(1)}, u32[]{:S(2)}, u32[]{:S(2)}) collective-permute-start(f32[12,2,8,128]{3,2,1,0:T(8,128)S(1)} %get-tuple-element.185), channel_id=1, source_target_pairs={{0,12},{1,13},{2,14},{3,15},{4,8},{5,9},{6,10},{7,11},{8,4},{9,5},... | collective-permute-start | bytes 294920 | tf_op jit(solution)/shard_map/cond/branch_3_fun/ppermute | solution.py:332
  82.5 25.0 %collective-permute-start.50 = (f32[12,2,8,128]{3,2,1,0:T(8,128)S(1)}, f32[12,2,8,128]{3,2,1,0:T(8,128)S(1)}, u32[]{:S(2)}, u32[]{:S(2)}) collective-permute-start(f32[12,2,8,128]{3,2,1,0:T(8,128)S(1)} %get-tuple-element.186), channel_id=1, source_target_pairs={{0,13},{1,12},{2,15},{3,14},{4,9},{5,8},{6,11},{7,10},{8,5},{9,4},... | collective-permute-start | bytes 294920 | tf_op jit(solution)/shard_map/cond/branch_3_fun/ppermute | solution.py:332
  90.6 19.4 %collective-permute-start.51 = (f32[12,2,8,128]{3,2,1,0:T(8,128)S(1)}, f32[12,2,8,128]{3,2,1,0:T(8,128)S(1)}, u32[]{:S(2)}, u32[]{:S(2)}) collective-permute-start(f32[12,2,8,128]{3,2,1,0:T(8,128)S(1)} %get-tuple-element.187), channel_id=1, source_target_pairs={{0,14},{1,15},{2,12},{3,13},{4,10},{5,11},{6,8},{7,9},{8,6},{9,7},... | collective-permute-start | bytes 294920 | tf_op jit(solution)/shard_map/cond/branch_3_fun/ppermute | solution.py:332
  92.7 20.1 %collective-permute-start.52 = (f32[12,2,8,128]{3,2,1,0:T(8,128)S(1)}, f32[12,2,8,128]{3,2,1,0:T(8,128)S(1)}, u32[]{:S(2)}, u32[]{:S(2)}) collective-permute-start(f32[12,2,8,128]{3,2,1,0:T(8,128)S(1)} %get-tuple-element.188), channel_id=1, source_target_pairs={{0,15},{1,14},{2,13},{3,12},{4,11},{5,10},{6,9},{7,8},{8,7},{9,6},... | collective-permute-start | bytes 294920 | tf_op jit(solution)/shard_map/cond/branch_3_fun/ppermute | solution.py:332
  96.9 16.7 %collective-permute-start.53 = (f32[12,2,8,128]{3,2,1,0:T(8,128)S(1)}, f32[12,2,8,128]{3,2,1,0:T(8,128)S(1)}, u32[]{:S(2)}, u32[]{:S(2)}) collective-permute-start(f32[12,2,8,128]{3,2,1,0:T(8,128)S(1)} %get-tuple-element.189), channel_id=1, source_target_pairs={{0,4},{1,5},{2,6},{3,7},{4,0},{5,1},{6,2},{7,3},{8,12},{9,13},{10,... | collective-permute-start | bytes 294920 | tf_op jit(solution)/shard_map/cond/branch_3_fun/ppermute | solution.py:332
  103.1 12.0 %collective-permute-start.54 = (f32[12,2,8,128]{3,2,1,0:T(8,128)S(1)}, f32[12,2,8,128]{3,2,1,0:T(8,128)S(1)}, u32[]{:S(2)}, u32[]{:S(2)}) collective-permute-start(f32[12,2,8,128]{3,2,1,0:T(8,128)S(1)} %get-tuple-element.190), channel_id=1, source_target_pairs={{0,5},{1,4},{2,7},{3,6},{4,1},{5,0},{6,3},{7,2},{8,13},{9,12},{10,... | collective-permute-start | bytes 294920 | tf_op jit(solution)/shard_map/cond/branch_3_fun/ppermute | solution.py:332
  107.5 7.8 %collective-permute-start.55 = (f32[12,2,8,128]{3,2,1,0:T(8,128)S(1)}, f32[12,2,8,128]{3,2,1,0:T(8,128)S(1)}, u32[]{:S(2)}, u32[]{:S(2)}) collective-permute-start(f32[12,2,8,128]{3,2,1,0:T(8,128)S(1)} %get-tuple-element.191), channel_id=1, source_target_pairs={{0,6},{1,7},{2,4},{3,5},{4,2},{5,3},{6,0},{7,1},{8,14},{9,15},{10,... | collective-permute-start | bytes 294920 | tf_op jit(solution)/shard_map/cond/branch_3_fun/ppermute | solution.py:332
  110.0 6.1 %collective-permute-start.56 = (f32[12,2,8,128]{3,2,1,0:T(8,128)S(1)}, f32[12,2,8,128]{3,2,1,0:T(8,128)S(1)}, u32[]{:S(2)}, u32[]{:S(2)}) collective-permute-start(f32[12,2,8,128]{3,2,1,0:T(8,128)S(1)} %get-tuple-element.192), channel_id=1, source_target_pairs={{0,7},{1,6},{2,5},{3,4},{4,3},{5,2},{6,1},{7,0},{8,15},{9,14},{10,... | collective-permute-start | bytes 294920 | tf_op jit(solution)/shard_map/cond/branch_3_fun/ppermute | solution.py:332
  112.8 5.3 %collective-permute-start.57 = (f32[12,2,8,128]{3,2,1,0:T(8,128)S(1)}, f32[12,2,8,128]{3,2,1,0:T(8,128)S(1)}, u32[]{:S(2)}, u32[]{:S(2)}) collective-permute-start(f32[12,2,8,128]{3,2,1,0:T(8,128)S(1)} %get-tuple-element.193), channel_id=1, source_target_pairs={{0,2},{1,3},{2,0},{3,1},{4,6},{5,7},{6,4},{7,5},{8,10},{9,11},{10,... | collective-permute-start | bytes 294920 | tf_op jit(solution)/shard_map/cond/branch_3_fun/ppermute | solution.py:332
  113.6 6.6 %collective-permute-start.58 = (f32[12,2,8,128]{3,2,1,0:T(8,128)S(1)}, f32[12,2,8,128]{3,2,1,0:T(8,128)S(1)}, u32[]{:S(2)}, u32[]{:S(2)}) collective-permute-start(f32[12,2,8,128]{3,2,1,0:T(8,128)S(1)} %get-tuple-element.194), channel_id=1, source_target_pairs={{0,3},{1,2},{2,1},{3,0},{4,7},{5,6},{6,5},{7,4},{8,11},{9,10},{10,... | collective-permute-start | bytes 294920 | tf_op jit(solution)/shard_map/cond/branch_3_fun/ppermute | solution.py:332
  115.1 5.1 %collective-permute-start.59 = (f32[12,2,8,128]{3,2,1,0:T(8,128)S(1)}, f32[12,2,8,128]{3,2,1,0:T(8,128)S(1)}, u32[]{:S(2)}, u32[]{:S(2)}) collective-permute-start(f32[12,2,8,128]{3,2,1,0:T(8,128)S(1)} %get-tuple-element.195), channel_id=1, source_target_pairs={{0,1},{1,0},{2,3},{3,2},{4,5},{5,4},{6,7},{7,6},{8,9},{9,8},{10,11... | collective-permute-start | bytes 294920 | tf_op jit(solution)/shard_map/cond/branch_3_fun/ppermute | solution.py:332
  (5 other events, 14.3 us)

commit v2 on v1

--- a/solution.py
+++ b/solution.py
@@ -249,11 +249,12 @@
                 out_ref[dev, block * halves + half, 1] = im
 
 
-def compact_kernel(slots, me_ref, index_ref, first_ref, second_ref, *outs):
+def compact_kernel(devices, slots, numbers, me_ref, index_ref, first_ref, second_ref, *outs):
     split = first_ref.shape[1]
     me = me_ref[0]
-    for number, (hop, out) in enumerate(zip(travel_order(len(outs)), outs)):
-        dev = me ^ hop
+    order = travel_order(devices)
+    for number, out in zip(numbers, outs):
+        dev = me ^ order[number]
         for slot in range(slots):
             index = index_ref[number, slot]
             early = first_ref[dev, jnp.minimum(index, split - 1)]
@@ -325,9 +326,10 @@
             cost_estimate=cost,
         )
 
-    def trade(values):
+    def trade(values, numbers=range(devices)):
         traded = []
-        for hop, value in zip(travel_order(devices), values):
+        for number, value in zip(numbers, values):
+            hop = travel_order(devices)[number]
             pairs = [(dev, dev ^ hop) for dev in range(devices)]
             traded.append(lax.ppermute(value, "col", pairs) if hop else value)
         return traded
@@ -405,18 +407,21 @@
 
     def finish(capacity):
         def run(me, index, own_place, weight, first, second):
-            sent = call(
-                functools.partial(compact_kernel, capacity),
-                [shape(capacity, 2, SUB, LANES)] * devices,
-                [SMEM_SPEC, SMEM_SPEC, VMEM_SPEC, VMEM_SPEC],
-            )(me, index, first, second)
+            sent = []
+            for numbers in (range(4), range(4, devices)):
+                packed = call(
+                    functools.partial(compact_kernel, devices, capacity, list(numbers)),
+                    [shape(capacity, 2, SUB, LANES)] * len(numbers),
+                    [SMEM_SPEC, SMEM_SPEC, VMEM_SPEC, VMEM_SPEC],
+                )(me, index, first, second)
+                sent += trade(packed, numbers)
             return call(
                 functools.partial(spread_kernel, devices),
                 shape(*slab.shape),
                 [SMEM_SPEC] * 3 + [VMEM_SPEC] * devices,
                 [pltpu.VMEM(slab.shape, jnp.float32), pltpu.SemaphoreType.DMA((blocks,))],
                 out_spec=HBM_SPEC,
-            )(me, own_place, weight, *trade(sent))
+            )(me, own_place, weight, *sent)
 
         return run
 

time: 123 us -> 123 us (level)
  starting transfers between devices: 55.7 us -> 54.4 us
    ppermute x30, starting transfers between devices: 49.2 us -> 47.8 us  [trade(): traded.append(lax.ppermute(value, 'col', pairs) if hop else value)]
  transfers between devices with their start and end apart: 31 -> 31, of which waited for: 19 -> 19; matrix products, arithmetic and copies ran while one was open for 2% -> 2% of each run, Pallas kernels for 6% -> 7%
where the time goes in v2:
time: 123 us; the launch traced here: 122 us
  starting transfers between devices  54.4 us (44%)
  waiting for transfers between devices  48.4 us (39%)
  Pallas kernels  13.2 us (11%)
  other arithmetic  2.63 us (2%)
  local copies, waits for them, and re-layouts  2.16 us (2%)
    ppermute x30, waiting for transfers between devices, trade(): traded.append(lax.ppermute(value, 'col', pairs) if hop else value)  48.4 us
    ppermute x30, starting transfers between devices, trade(): traded.append(lax.ppermute(value, 'col', pairs) if hop else value)  47.8 us
    pallas_call x2, Pallas kernels, transform(): call(functools.partial(transform_kernel, devices, count, masks), outs, [V...  6.64 us
    all_to_all x1, starting transfers between devices, shards_tiled(): lax.all_to_all(message, 'col', split_axis=0, concat_axis=0, tiled=True)  6.53 us
  transfers between devices with their start and end apart: 31, of which 19 were waited for; matrix products, arithmetic and copies ran while one was open for 2% of the time, Pallas kernels for 7%

profile of v2, /device:TPU:13, one launch (start us, length us, event | category | flops | bytes accessed | tf_op | source)
XLA Modules:
  0.0 121.8 jit_solution(9401682704772013750)
XLA Ops:
  0.0 1.6 %copy-done = f32[2,1024,256]{2,1,0:T(8,128)S(1)} copy-done((f32[2,1024,256]{2,1,0:T(8,128)S(1)}, f32[2,1024,256]{2,1,0:T(8,128)}, u32[]{:S(2)}) %copy-start) | copy-done | bytes 2097176
  2.6 6.5 %all-to-all-start = ((f32[16,8,8,128]{3,2,1,0:T(8,128)}), f32[16,8,8,128]{3,2,1,0:T(8,128)S(1)}, u32[]{:S(2)}, u32[]{:S(2)}) async-start(f32[16,8,8,128]{3,2,1,0:T(8,128)} %shard_map.69), calls=%async_computation | async-start | bytes 1048576 | tf_op jit(solution)/shard_map/all_to_all | solution.py:357
  9.3 1.4 %shard_map.67 = (f32[25,8,128]{2,1,0:T(8,128)S(1)}, f32[25,8,128]{2,1,0:T(8,128)S(1)}, f32[25,8,128]{2,1,0:T(8,128)S(1)}, f32[25,8,128]{2,1,0:T(8,128)S(1)}, f32...) custom-call(s32[1]{0:T(128)} %bitcast.7.me_ref, ...), custom_call_target="tpu_custom_call" | custom-call | tf_op jit(solution)/shard_map/pallas_call | solution.py:343
  10.7 2.2 %collective-permute-start.105 = (f32[25,8,128]{2,1,0:T(8,128)S(1)}, f32[25,8,128]{2,1,0:T(8,128)S(1)}, u32[]{:S(2)}, u32[]{:S(2)}) collective-permute-start(f32[25,8,128]{2,1,0:T(8,128)S(1)} %get-tuple-element.283), channel_id=1, source_target_pairs={{0,8},{1,9},{2,10},{3,11},{4,12},{5,13},{6,14},{7,15},{8,0},{9,1},... | collective-permute-start | bytes 307208 | tf_op jit(solution)/shard_map/ppermute | solution.py:334
  13.7 2.1 %collective-permute-start.107 = (f32[25,8,128]{2,1,0:T(8,128)S(1)}, f32[25,8,128]{2,1,0:T(8,128)S(1)}, u32[]{:S(2)}, u32[]{:S(2)}) collective-permute-start(f32[25,8,128]{2,1,0:T(8,128)S(1)} %get-tuple-element.285), channel_id=1, source_target_pairs={{0,10},{1,11},{2,8},{3,9},{4,14},{5,15},{6,12},{7,13},{8,2},{9,3},... | collective-permute-start | bytes 307208 | tf_op jit(solution)/shard_map/ppermute | solution.py:334
  20.7 13.1 %collective-permute-done.105.refs_0_ = f32[25,8,128]{2,1,0:T(8,128)S(1)} collective-permute-done((f32[25,8,128]{2,1,0:T(8,128)S(1)}, f32[25,8,128]{2,1,0:T(8,128)S(1)}, u32[]{:S(2)}, u32[]{:S(2)}) %collective-permute-start.105) | collective-permute-done | bytes 102432 | tf_op jit(solution)/shard_map/ppermute | solution.py:334
  33.8 2.5 %collective-permute-start.110 = (f32[25,8,128]{2,1,0:T(8,128)S(1)}, f32[25,8,128]{2,1,0:T(8,128)S(1)}, u32[]{:S(2)}, u32[]{:S(2)}) collective-permute-start(f32[25,8,128]{2,1,0:T(8,128)S(1)} %get-tuple-element.288), channel_id=1, source_target_pairs={{0,13},{1,12},{2,15},{3,14},{4,9},{5,8},{6,11},{7,10},{8,5},{9,4},... | collective-permute-start | bytes 307208 | tf_op jit(solution)/shard_map/ppermute | solution.py:334
  38.2 2.4 %collective-permute-start.112 = (f32[25,8,128]{2,1,0:T(8,128)S(1)}, f32[25,8,128]{2,1,0:T(8,128)S(1)}, u32[]{:S(2)}, u32[]{:S(2)}) collective-permute-start(f32[25,8,128]{2,1,0:T(8,128)S(1)} %get-tuple-element.290), channel_id=1, source_target_pairs={{0,15},{1,14},{2,13},{3,12},{4,11},{5,10},{6,9},{7,8},{8,7},{9,6},... | collective-permute-start | bytes 307208 | tf_op jit(solution)/shard_map/ppermute | solution.py:334
  40.5 4.2 %collective-permute-done.108.refs_3_ = f32[25,8,128]{2,1,0:T(8,128)S(1)} collective-permute-done((f32[25,8,128]{2,1,0:T(8,128)S(1)}, f32[25,8,128]{2,1,0:T(8,128)S(1)}, u32[]{:S(2)}, u32[]{:S(2)}) %collective-permute-start.108) | collective-permute-done | bytes 102432 | tf_op jit(solution)/shard_map/ppermute | solution.py:334
  44.7 4.2 %collective-permute-start.113 = (f32[25,8,128]{2,1,0:T(8,128)S(1)}, f32[25,8,128]{2,1,0:T(8,128)S(1)}, u32[]{:S(2)}, u32[]{:S(2)}) collective-permute-start(f32[25,8,128]{2,1,0:T(8,128)S(1)} %get-tuple-element.291), channel_id=1, source_target_pairs={{0,4},{1,5},{2,6},{3,7},{4,0},{5,1},{6,2},{7,3},{8,12},{9,13},{10,... | collective-permute-start | bytes 307208 | tf_op jit(solution)/shard_map/ppermute | solution.py:334
  49.9 4.3 %collective-permute-done.110.refs_5_ = f32[25,8,128]{2,1,0:T(8,128)S(1)} collective-permute-done((f32[25,8,128]{2,1,0:T(8,128)S(1)}, f32[25,8,128]{2,1,0:T(8,128)S(1)}, u32[]{:S(2)}, u32[]{:S(2)}) %collective-permute-start.110) | collective-permute-done | bytes 102432 | tf_op jit(solution)/shard_map/ppermute | solution.py:334
  55.9 2.4 %collective-permute-done.112.refs_7_ = f32[25,8,128]{2,1,0:T(8,128)S(1)} collective-permute-done((f32[25,8,128]{2,1,0:T(8,128)S(1)}, f32[25,8,128]{2,1,0:T(8,128)S(1)}, u32[]{:S(2)}, u32[]{:S(2)}) %collective-permute-start.112) | collective-permute-done | bytes 102432 | tf_op jit(solution)/shard_map/ppermute | solution.py:334
  58.4 2.0 %collective-permute-start.117 = (f32[25,8,128]{2,1,0:T(8,128)S(1)}, f32[25,8,128]{2,1,0:T(8,128)S(1)}, u32[]{:S(2)}, u32[]{:S(2)}) collective-permute-start(f32[25,8,128]{2,1,0:T(8,128)S(1)} %get-tuple-element.295), channel_id=1, source_target_pairs={{0,2},{1,3},{2,0},{3,1},{4,6},{5,7},{6,4},{7,5},{8,10},{9,11},{10,... | collective-permute-start | bytes 307208 | tf_op jit(solution)/shard_map/ppermute | solution.py:334
  60.8 1.2 %collective-permute-done.116.refs_11_ = f32[25,8,128]{2,1,0:T(8,128)S(1)} collective-permute-done((f32[25,8,128]{2,1,0:T(8,128)S(1)}, f32[25,8,128]{2,1,0:T(8,128)S(1)}, u32[]{:S(2)}, u32[]{:S(2)}) %collective-permute-start.116) | collective-permute-done | bytes 102432 | tf_op jit(solution)/shard_map/ppermute | solution.py:334
  62.0 2.6 %collective-permute-done.117.refs_12_ = f32[25,8,128]{2,1,0:T(8,128)S(1)} collective-permute-done((f32[25,8,128]{2,1,0:T(8,128)S(1)}, f32[25,8,128]{2,1,0:T(8,128)S(1)}, u32[]{:S(2)}, u32[]{:S(2)}) %collective-permute-start.117) | collective-permute-done | bytes 102432 | tf_op jit(solution)/shard_map/ppermute | solution.py:334
  64.6 2.2 %collective-permute-done.118.refs_13_ = f32[25,8,128]{2,1,0:T(8,128)S(1)} collective-permute-done((f32[25,8,128]{2,1,0:T(8,128)S(1)}, f32[25,8,128]{2,1,0:T(8,128)S(1)}, u32[]{:S(2)}, u32[]{:S(2)}) %collective-permute-start.118) | collective-permute-done | bytes 102432 | tf_op jit(solution)/shard_map/ppermute | solution.py:334
  66.8 5.5 %shard_map.68 = (f32[16,12,2,8,128]{4,3,2,1,0:T(8,128)}, s32[16,128]{1,0:T(8,128)S(1)}, s32[16,128]{1,0:T(8,128)S(1)}, s32[1]{0:T(128)}) custom-call(f32[512,512]{1,0:T(8,128)S(1)} %maximum_maximum_fusion.table_ref, f32[16,512]{1,0:T(8,128)S(1)} %pad_maximum_fusion.twiddle_ref, f32[25,8,128]{2,1,0:T(8,128)S(1)} %collective-permute-done.105.refs_0_, ...), custom_call_target="tpu_custom_call" | custom-call | flops 1207959552 | bytes 16777216 | tf_op jit(solution)/shard_map/pallas_call | solution.py:386
  74.3 47.3 %conditional.1 = (f32[2,1024,256]{2,1,0:T(8,128)}) conditional(s32[]{:T(128)} %bitcast.9, (s32[1]{0:T(128)}, s32[16,128]{1,0:T(8,128)S(1)}, f32[16,12,2,8,128]{4,3,2,1,0:T(8,128)S(1)}, f32[16,4,2,8,128]{4,3,2,1,0:T(8,128)S(1)}, s32[16,128]{1,0:T(8,128)S(1)}, /*index=5*/f32[8,2]{0,1:T(2,128)S(1)}, (), ...), branch_computations={%region_1.2_spmd, %region_2.3_spmd, %region_3.4_spmd, %region_4.5_... | conditional | flops 208 | bytes 7865912 | solution.py:446
  75.3 2.9 %collective-permute-start.46 = (f32[12,2,8,128]{3,2,1,0:T(8,128)S(1)}, f32[12,2,8,128]{3,2,1,0:T(8,128)S(1)}, u32[]{:S(2)}, u32[]{:S(2)}) collective-permute-start(f32[12,2,8,128]{3,2,1,0:T(8,128)S(1)} %get-tuple-element.182), channel_id=1, source_target_pairs={{0,9},{1,8},{2,11},{3,10},{4,13},{5,12},{6,15},{7,14},{8,1},{9,0},... | collective-permute-start | bytes 294920 | tf_op jit(solution)/shard_map/cond/branch_3_fun/ppermute | solution.py:334
  79.0 2.5 %collective-permute-start.48 = (f32[12,2,8,128]{3,2,1,0:T(8,128)S(1)}, f32[12,2,8,128]{3,2,1,0:T(8,128)S(1)}, u32[]{:S(2)}, u32[]{:S(2)}) collective-permute-start(f32[12,2,8,128]{3,2,1,0:T(8,128)S(1)} %get-tuple-element.184), channel_id=1, source_target_pairs={{0,11},{1,10},{2,9},{3,8},{4,15},{5,14},{6,13},{7,12},{8,3},{9,2},... | collective-permute-start | bytes 294920 | tf_op jit(solution)/shard_map/cond/branch_3_fun/ppermute | solution.py:334
  81.5 1.3 %branch_3_fun.4 = (f32[12,2,8,128]{3,2,1,0:T(8,128)S(1)}, f32[12,2,8,128]{3,2,1,0:T(8,128)S(1)}, f32[12,2,8,128]{3,2,1,0:T(8,128)S(1)}, f32[12,2,8,128]{3,2,1,0:...) custom-call(s32[1]{0:T(128)} %get-tuple-element.175.me_ref, ...), custom_call_target="tpu_custom_call" | custom-call | tf_op jit(solution)/shard_map/cond/branch_3_fun/pallas_call | solution.py:412
  83.2 6.5 %collective-permute-start.50 = (f32[12,2,8,128]{3,2,1,0:T(8,128)S(1)}, f32[12,2,8,128]{3,2,1,0:T(8,128)S(1)}, u32[]{:S(2)}, u32[]{:S(2)}) collective-permute-start(f32[12,2,8,128]{3,2,1,0:T(8,128)S(1)} %get-tuple-element.186), channel_id=1, source_target_pairs={{0,13},{1,12},{2,15},{3,14},{4,9},{5,8},{6,11},{7,10},{8,5},{9,4},... | collective-permute-start | bytes 294920 | tf_op jit(solution)/shard_map/cond/branch_3_fun/ppermute | solution.py:334
  90.0 1.8 %collective-permute-start.51 = (f32[12,2,8,128]{3,2,1,0:T(8,128)S(1)}, f32[12,2,8,128]{3,2,1,0:T(8,128)S(1)}, u32[]{:S(2)}, u32[]{:S(2)}) collective-permute-start(f32[12,2,8,128]{3,2,1,0:T(8,128)S(1)} %get-tuple-element.187), channel_id=1, source_target_pairs={{0,14},{1,15},{2,12},{3,13},{4,10},{5,11},{6,8},{7,9},{8,6},{9,7},... | collective-permute-start | bytes 294920 | tf_op jit(solution)/shard_map/cond/branch_3_fun/ppermute | solution.py:334
  92.1 4.2 %collective-permute-start.52 = (f32[12,2,8,128]{3,2,1,0:T(8,128)S(1)}, f32[12,2,8,128]{3,2,1,0:T(8,128)S(1)}, u32[]{:S(2)}, u32[]{:S(2)}) collective-permute-start(f32[12,2,8,128]{3,2,1,0:T(8,128)S(1)} %get-tuple-element.188), channel_id=1, source_target_pairs={{0,15},{1,14},{2,13},{3,12},{4,11},{5,10},{6,9},{7,8},{8,7},{9,6},... | collective-permute-start | bytes 294920 | tf_op jit(solution)/shard_map/cond/branch_3_fun/ppermute | solution.py:334
  96.3 5.8 %collective-permute-start.53 = (f32[12,2,8,128]{3,2,1,0:T(8,128)S(1)}, f32[12,2,8,128]{3,2,1,0:T(8,128)S(1)}, u32[]{:S(2)}, u32[]{:S(2)}) collective-permute-start(f32[12,2,8,128]{3,2,1,0:T(8,128)S(1)} %get-tuple-element.189), channel_id=1, source_target_pairs={{0,4},{1,5},{2,6},{3,7},{4,0},{5,1},{6,2},{7,3},{8,12},{9,13},{10,... | collective-permute-start | bytes 294920 | tf_op jit(solution)/shard_map/cond/branch_3_fun/ppermute | solution.py:334
  102.8 4.1 %collective-permute-done.50.refs_5_ = f32[12,2,8,128]{3,2,1,0:T(8,128)S(1)} collective-permute-done((f32[12,2,8,128]{3,2,1,0:T(8,128)S(1)}, f32[12,2,8,128]{3,2,1,0:T(8,128)S(1)}, u32[]{:S(2)}, u32[]{:S(2)}) %collective-permute-start.50) | collective-permute-done | bytes 98336 | tf_op jit(solution)/shard_map/cond/branch_3_fun/ppermute | solution.py:334
  107.1 2.3 %collective-permute-done.51.refs_6_ = f32[12,2,8,128]{3,2,1,0:T(8,128)S(1)} collective-permute-done((f32[12,2,8,128]{3,2,1,0:T(8,128)S(1)}, f32[12,2,8,128]{3,2,1,0:T(8,128)S(1)}, u32[]{:S(2)}, u32[]{:S(2)}) %collective-permute-start.51) | collective-permute-done | bytes 98336 | tf_op jit(solution)/shard_map/cond/branch_3_fun/ppermute | solution.py:334
  109.4 2.8 %collective-permute-done.52.refs_7_ = f32[12,2,8,128]{3,2,1,0:T(8,128)S(1)} collective-permute-done((f32[12,2,8,128]{3,2,1,0:T(8,128)S(1)}, f32[12,2,8,128]{3,2,1,0:T(8,128)S(1)}, u32[]{:S(2)}, u32[]{:S(2)}) %collective-permute-start.52) | collective-permute-done | bytes 98336 | tf_op jit(solution)/shard_map/cond/branch_3_fun/ppermute | solution.py:334
  113.0 1.5 %collective-permute-start.58 = (f32[12,2,8,128]{3,2,1,0:T(8,128)S(1)}, f32[12,2,8,128]{3,2,1,0:T(8,128)S(1)}, u32[]{:S(2)}, u32[]{:S(2)}) collective-permute-start(f32[12,2,8,128]{3,2,1,0:T(8,128)S(1)} %get-tuple-element.194), channel_id=1, source_target_pairs={{0,3},{1,2},{2,1},{3,0},{4,7},{5,6},{6,5},{7,4},{8,11},{9,10},{10,... | collective-permute-start | bytes 294920 | tf_op jit(solution)/shard_map/cond/branch_3_fun/ppermute | solution.py:334
  115.5 2.0 %collective-permute-done.57.refs_12_ = f32[12,2,8,128]{3,2,1,0:T(8,128)S(1)} collective-permute-done((f32[12,2,8,128]{3,2,1,0:T(8,128)S(1)}, f32[12,2,8,128]{3,2,1,0:T(8,128)S(1)}, u32[]{:S(2)}, u32[]{:S(2)}) %collective-permute-start.57) | collective-permute-done | bytes 98336 | tf_op jit(solution)/shard_map/cond/branch_3_fun/ppermute | solution.py:334
  117.5 2.1 %collective-permute-done.58.refs_13_ = f32[12,2,8,128]{3,2,1,0:T(8,128)S(1)} collective-permute-done((f32[12,2,8,128]{3,2,1,0:T(8,128)S(1)}, f32[12,2,8,128]{3,2,1,0:T(8,128)S(1)}, u32[]{:S(2)}, u32[]{:S(2)}) %collective-permute-start.58) | collective-permute-done | bytes 98336 | tf_op jit(solution)/shard_map/cond/branch_3_fun/ppermute | solution.py:334
  119.6 2.0 %branch_3_fun.5 = f32[2,1024,256]{2,1,0:T(8,128)} custom-call(s32[1]{0:T(128)} %get-tuple-element.175.me_ref, s32[16]{0:T(128)S(1)} %slice_bitcast_fusion.3.slot_ref, f32[16]{0:T(128)S(1)} %reshape.84.weight_ref, f32[12,2,8,128]{3,2,1,0:T(8,128)S(1)} %collective-permute-done.45.refs_0_, f32[12,2,8,128]{3,2,1,0:T(8,128)S(1)} %collective-permute-done.46.refs_1_, ...), custom_call_target="tpu_custom_call" | custom-call | tf_op jit(solution)/shard_map/cond/branch_3_fun/pallas_call | solution.py:418
  (68 shorter events, 18.5 us)
Async XLA Ops:
  0.0 9.1 %copy-start.5 = (s32[8,2]{0,1:T(2,128)S(1)}, s32[8,2]{0,1:T(2,128)}, u32[]{:S(2)}) copy-start(s32[8,2]{0,1:T(2,128)} %param.14) | copy-start | bytes 196
  2.6 70.4 %all-to-all-start = ((f32[16,8,8,128]{3,2,1,0:T(8,128)}), f32[16,8,8,128]{3,2,1,0:T(8,128)S(1)}, u32[]{:S(2)}, u32[]{:S(2)}) async-start(f32[16,8,8,128]{3,2,1,0:T(8,128)} %shard_map.69), calls=%async_computation | async-start | bytes 1048576 | tf_op jit(solution)/shard_map/all_to_all | solution.py:357
  10.7 23.0 %collective-permute-start.105 = (f32[25,8,128]{2,1,0:T(8,128)S(1)}, f32[25,8,128]{2,1,0:T(8,128)S(1)}, u32[]{:S(2)}, u32[]{:S(2)}) collective-permute-start(f32[25,8,128]{2,1,0:T(8,128)S(1)} %get-tuple-element.283), channel_id=1, source_target_pairs={{0,8},{1,9},{2,10},{3,11},{4,12},{5,13},{6,14},{7,15},{8,0},{9,1},... | collective-permute-start | bytes 307208 | tf_op jit(solution)/shard_map/ppermute | solution.py:334
  12.9 23.4 %collective-permute-start.106 = (f32[25,8,128]{2,1,0:T(8,128)S(1)}, f32[25,8,128]{2,1,0:T(8,128)S(1)}, u32[]{:S(2)}, u32[]{:S(2)}) collective-permute-start(f32[25,8,128]{2,1,0:T(8,128)S(1)} %get-tuple-element.284), channel_id=1, source_target_pairs={{0,9},{1,8},{2,11},{3,10},{4,13},{5,12},{6,15},{7,14},{8,1},{9,0},... | collective-permute-start | bytes 307208 | tf_op jit(solution)/shard_map/ppermute | solution.py:334
  13.7 24.4 %collective-permute-start.107 = (f32[25,8,128]{2,1,0:T(8,128)S(1)}, f32[25,8,128]{2,1,0:T(8,128)S(1)}, u32[]{:S(2)}, u32[]{:S(2)}) collective-permute-start(f32[25,8,128]{2,1,0:T(8,128)S(1)} %get-tuple-element.285), channel_id=1, source_target_pairs={{0,10},{1,11},{2,8},{3,9},{4,14},{5,15},{6,12},{7,13},{8,2},{9,3},... | collective-permute-start | bytes 307208 | tf_op jit(solution)/shard_map/ppermute | solution.py:334
  15.8 28.9 %collective-permute-start.108 = (f32[25,8,128]{2,1,0:T(8,128)S(1)}, f32[25,8,128]{2,1,0:T(8,128)S(1)}, u32[]{:S(2)}, u32[]{:S(2)}) collective-permute-start(f32[25,8,128]{2,1,0:T(8,128)S(1)} %get-tuple-element.286), channel_id=1, source_target_pairs={{0,11},{1,10},{2,9},{3,8},{4,15},{5,14},{6,13},{7,12},{8,3},{9,2},... | collective-permute-start | bytes 307208 | tf_op jit(solution)/shard_map/ppermute | solution.py:334
  17.0 32.8 %collective-permute-start.109 = (f32[25,8,128]{2,1,0:T(8,128)S(1)}, f32[25,8,128]{2,1,0:T(8,128)S(1)}, u32[]{:S(2)}, u32[]{:S(2)}) collective-permute-start(f32[25,8,128]{2,1,0:T(8,128)S(1)} %get-tuple-element.287), channel_id=1, source_target_pairs={{0,12},{1,13},{2,14},{3,15},{4,8},{5,9},{6,10},{7,11},{8,4},{9,5},... | collective-permute-start | bytes 307208 | tf_op jit(solution)/shard_map/ppermute | solution.py:334
  33.8 20.5 %collective-permute-start.110 = (f32[25,8,128]{2,1,0:T(8,128)S(1)}, f32[25,8,128]{2,1,0:T(8,128)S(1)}, u32[]{:S(2)}, u32[]{:S(2)}) collective-permute-start(f32[25,8,128]{2,1,0:T(8,128)S(1)} %get-tuple-element.288), channel_id=1, source_target_pairs={{0,13},{1,12},{2,15},{3,14},{4,9},{5,8},{6,11},{7,10},{8,5},{9,4},... | collective-permute-start | bytes 307208 | tf_op jit(solution)/shard_map/ppermute | solution.py:334
  36.3 19.1 %collective-permute-start.111 = (f32[25,8,128]{2,1,0:T(8,128)S(1)}, f32[25,8,128]{2,1,0:T(8,128)S(1)}, u32[]{:S(2)}, u32[]{:S(2)}) collective-permute-start(f32[25,8,128]{2,1,0:T(8,128)S(1)} %get-tuple-element.289), channel_id=1, source_target_pairs={{0,14},{1,15},{2,12},{3,13},{4,10},{5,11},{6,8},{7,9},{8,6},{9,7},... | collective-permute-start | bytes 307208 | tf_op jit(solution)/shard_map/ppermute | solution.py:334
  38.2 20.2 %collective-permute-start.112 = (f32[25,8,128]{2,1,0:T(8,128)S(1)}, f32[25,8,128]{2,1,0:T(8,128)S(1)}, u32[]{:S(2)}, u32[]{:S(2)}) collective-permute-start(f32[25,8,128]{2,1,0:T(8,128)S(1)} %get-tuple-element.290), channel_id=1, source_target_pairs={{0,15},{1,14},{2,13},{3,12},{4,11},{5,10},{6,9},{7,8},{8,7},{9,6},... | collective-permute-start | bytes 307208 | tf_op jit(solution)/shard_map/ppermute | solution.py:334
  44.7 15.6 %collective-permute-start.113 = (f32[25,8,128]{2,1,0:T(8,128)S(1)}, f32[25,8,128]{2,1,0:T(8,128)S(1)}, u32[]{:S(2)}, u32[]{:S(2)}) collective-permute-start(f32[25,8,128]{2,1,0:T(8,128)S(1)} %get-tuple-element.291), channel_id=1, source_target_pairs={{0,4},{1,5},{2,6},{3,7},{4,0},{5,1},{6,2},{7,3},{8,12},{9,13},{10,... | collective-permute-start | bytes 307208 | tf_op jit(solution)/shard_map/ppermute | solution.py:334
  49.8 10.6 %collective-permute-start.114 = (f32[25,8,128]{2,1,0:T(8,128)S(1)}, f32[25,8,128]{2,1,0:T(8,128)S(1)}, u32[]{:S(2)}, u32[]{:S(2)}) collective-permute-start(f32[25,8,128]{2,1,0:T(8,128)S(1)} %get-tuple-element.292), channel_id=1, source_target_pairs={{0,5},{1,4},{2,7},{3,6},{4,1},{5,0},{6,3},{7,2},{8,13},{9,12},{10,... | collective-permute-start | bytes 307208 | tf_op jit(solution)/shard_map/ppermute | solution.py:334
  54.3 6.5 %collective-permute-start.115 = (f32[25,8,128]{2,1,0:T(8,128)S(1)}, f32[25,8,128]{2,1,0:T(8,128)S(1)}, u32[]{:S(2)}, u32[]{:S(2)}) collective-permute-start(f32[25,8,128]{2,1,0:T(8,128)S(1)} %get-tuple-element.293), channel_id=1, source_target_pairs={{0,6},{1,7},{2,4},{3,5},{4,2},{5,3},{6,0},{7,1},{8,14},{9,15},{10,... | collective-permute-start | bytes 307208 | tf_op jit(solution)/shard_map/ppermute | solution.py:334
  55.3 6.7 %collective-permute-start.116 = (f32[25,8,128]{2,1,0:T(8,128)S(1)}, f32[25,8,128]{2,1,0:T(8,128)S(1)}, u32[]{:S(2)}, u32[]{:S(2)}) collective-permute-start(f32[25,8,128]{2,1,0:T(8,128)S(1)} %get-tuple-element.294), channel_id=1, source_target_pairs={{0,7},{1,6},{2,5},{3,4},{4,3},{5,2},{6,1},{7,0},{8,15},{9,14},{10,... | collective-permute-start | bytes 307208 | tf_op jit(solution)/shard_map/ppermute | solution.py:334
  58.4 6.2 %collective-permute-start.117 = (f32[25,8,128]{2,1,0:T(8,128)S(1)}, f32[25,8,128]{2,1,0:T(8,128)S(1)}, u32[]{:S(2)}, u32[]{:S(2)}) collective-permute-start(f32[25,8,128]{2,1,0:T(8,128)S(1)} %get-tuple-element.295), channel_id=1, source_target_pairs={{0,2},{1,3},{2,0},{3,1},{4,6},{5,7},{6,4},{7,5},{8,10},{9,11},{10,... | collective-permute-start | bytes 307208 | tf_op jit(solution)/shard_map/ppermute | solution.py:334
  60.4 6.5 %collective-permute-start.118 = (f32[25,8,128]{2,1,0:T(8,128)S(1)}, f32[25,8,128]{2,1,0:T(8,128)S(1)}, u32[]{:S(2)}, u32[]{:S(2)}) collective-permute-start(f32[25,8,128]{2,1,0:T(8,128)S(1)} %get-tuple-element.296), channel_id=1, source_target_pairs={{0,3},{1,2},{2,1},{3,0},{4,7},{5,6},{6,5},{7,4},{8,11},{9,10},{10,... | collective-permute-start | bytes 307208 | tf_op jit(solution)/shard_map/ppermute | solution.py:334
  60.4 6.5 %collective-permute-start.119 = (f32[25,8,128]{2,1,0:T(8,128)S(1)}, f32[25,8,128]{2,1,0:T(8,128)S(1)}, u32[]{:S(2)}, u32[]{:S(2)}) collective-permute-start(f32[25,8,128]{2,1,0:T(8,128)S(1)} %get-tuple-element.297), channel_id=1, source_target_pairs={{0,1},{1,0},{2,3},{3,2},{4,5},{5,4},{6,7},{7,6},{8,9},{9,8},{10,11... | collective-permute-start | bytes 307208 | tf_op jit(solution)/shard_map/ppermute | solution.py:334
  75.3 8.0 %collective-permute-start.45 = (f32[12,2,8,128]{3,2,1,0:T(8,128)S(1)}, f32[12,2,8,128]{3,2,1,0:T(8,128)S(1)}, u32[]{:S(2)}, u32[]{:S(2)}) collective-permute-start(f32[12,2,8,128]{3,2,1,0:T(8,128)S(1)} %get-tuple-element.181), channel_id=1, source_target_pairs={{0,8},{1,9},{2,10},{3,11},{4,12},{5,13},{6,14},{7,15},{8,0},{9,1},... | collective-permute-start | bytes 294920 | tf_op jit(solution)/shard_map/cond/branch_3_fun/ppermute | solution.py:334
  75.3 14.6 %collective-permute-start.46 = (f32[12,2,8,128]{3,2,1,0:T(8,128)S(1)}, f32[12,2,8,128]{3,2,1,0:T(8,128)S(1)}, u32[]{:S(2)}, u32[]{:S(2)}) collective-permute-start(f32[12,2,8,128]{3,2,1,0:T(8,128)S(1)} %get-tuple-element.182), channel_id=1, source_target_pairs={{0,9},{1,8},{2,11},{3,10},{4,13},{5,12},{6,15},{7,14},{8,1},{9,0},... | collective-permute-start | bytes 294920 | tf_op jit(solution)/shard_map/cond/branch_3_fun/ppermute | solution.py:334
  78.3 13.8 %collective-permute-start.47 = (f32[12,2,8,128]{3,2,1,0:T(8,128)S(1)}, f32[12,2,8,128]{3,2,1,0:T(8,128)S(1)}, u32[]{:S(2)}, u32[]{:S(2)}) collective-permute-start(f32[12,2,8,128]{3,2,1,0:T(8,128)S(1)} %get-tuple-element.183), channel_id=1, source_target_pairs={{0,10},{1,11},{2,8},{3,9},{4,14},{5,15},{6,12},{7,13},{8,2},{9,3},... | collective-permute-start | bytes 294920 | tf_op jit(solution)/shard_map/cond/branch_3_fun/ppermute | solution.py:334
  79.0 17.3 %collective-permute-start.48 = (f32[12,2,8,128]{3,2,1,0:T(8,128)S(1)}, f32[12,2,8,128]{3,2,1,0:T(8,128)S(1)}, u32[]{:S(2)}, u32[]{:S(2)}) collective-permute-start(f32[12,2,8,128]{3,2,1,0:T(8,128)S(1)} %get-tuple-element.184), channel_id=1, source_target_pairs={{0,11},{1,10},{2,9},{3,8},{4,15},{5,14},{6,13},{7,12},{8,3},{9,2},... | collective-permute-start | bytes 294920 | tf_op jit(solution)/shard_map/cond/branch_3_fun/ppermute | solution.py:334
  82.8 19.7 %collective-permute-start.49 = (f32[12,2,8,128]{3,2,1,0:T(8,128)S(1)}, f32[12,2,8,128]{3,2,1,0:T(8,128)S(1)}, u32[]{:S(2)}, u32[]{:S(2)}) collective-permute-start(f32[12,2,8,128]{3,2,1,0:T(8,128)S(1)} %get-tuple-element.185), channel_id=1, source_target_pairs={{0,12},{1,13},{2,14},{3,15},{4,8},{5,9},{6,10},{7,11},{8,4},{9,5},... | collective-permute-start | bytes 294920 | tf_op jit(solution)/shard_map/cond/branch_3_fun/ppermute | solution.py:334
  83.2 23.7 %collective-permute-start.50 = (f32[12,2,8,128]{3,2,1,0:T(8,128)S(1)}, f32[12,2,8,128]{3,2,1,0:T(8,128)S(1)}, u32[]{:S(2)}, u32[]{:S(2)}) collective-permute-start(f32[12,2,8,128]{3,2,1,0:T(8,128)S(1)} %get-tuple-element.186), channel_id=1, source_target_pairs={{0,13},{1,12},{2,15},{3,14},{4,9},{5,8},{6,11},{7,10},{8,5},{9,4},... | collective-permute-start | bytes 294920 | tf_op jit(solution)/shard_map/cond/branch_3_fun/ppermute | solution.py:334
  90.0 19.4 %collective-permute-start.51 = (f32[12,2,8,128]{3,2,1,0:T(8,128)S(1)}, f32[12,2,8,128]{3,2,1,0:T(8,128)S(1)}, u32[]{:S(2)}, u32[]{:S(2)}) collective-permute-start(f32[12,2,8,128]{3,2,1,0:T(8,128)S(1)} %get-tuple-element.187), channel_id=1, source_target_pairs={{0,14},{1,15},{2,12},{3,13},{4,10},{5,11},{6,8},{7,9},{8,6},{9,7},... | collective-permute-start | bytes 294920 | tf_op jit(solution)/shard_map/cond/branch_3_fun/ppermute | solution.py:334
  92.1 20.1 %collective-permute-start.52 = (f32[12,2,8,128]{3,2,1,0:T(8,128)S(1)}, f32[12,2,8,128]{3,2,1,0:T(8,128)S(1)}, u32[]{:S(2)}, u32[]{:S(2)}) collective-permute-start(f32[12,2,8,128]{3,2,1,0:T(8,128)S(1)} %get-tuple-element.188), channel_id=1, source_target_pairs={{0,15},{1,14},{2,13},{3,12},{4,11},{5,10},{6,9},{7,8},{8,7},{9,6},... | collective-permute-start | bytes 294920 | tf_op jit(solution)/shard_map/cond/branch_3_fun/ppermute | solution.py:334
  96.3 16.6 %collective-permute-start.53 = (f32[12,2,8,128]{3,2,1,0:T(8,128)S(1)}, f32[12,2,8,128]{3,2,1,0:T(8,128)S(1)}, u32[]{:S(2)}, u32[]{:S(2)}) collective-permute-start(f32[12,2,8,128]{3,2,1,0:T(8,128)S(1)} %get-tuple-element.189), channel_id=1, source_target_pairs={{0,4},{1,5},{2,6},{3,7},{4,0},{5,1},{6,2},{7,3},{8,12},{9,13},{10,... | collective-permute-start | bytes 294920 | tf_op jit(solution)/shard_map/cond/branch_3_fun/ppermute | solution.py:334
  102.5 12.0 %collective-permute-start.54 = (f32[12,2,8,128]{3,2,1,0:T(8,128)S(1)}, f32[12,2,8,128]{3,2,1,0:T(8,128)S(1)}, u32[]{:S(2)}, u32[]{:S(2)}) collective-permute-start(f32[12,2,8,128]{3,2,1,0:T(8,128)S(1)} %get-tuple-element.190), channel_id=1, source_target_pairs={{0,5},{1,4},{2,7},{3,6},{4,1},{5,0},{6,3},{7,2},{8,13},{9,12},{10,... | collective-permute-start | bytes 294920 | tf_op jit(solution)/shard_map/cond/branch_3_fun/ppermute | solution.py:334
  106.9 7.8 %collective-permute-start.55 = (f32[12,2,8,128]{3,2,1,0:T(8,128)S(1)}, f32[12,2,8,128]{3,2,1,0:T(8,128)S(1)}, u32[]{:S(2)}, u32[]{:S(2)}) collective-permute-start(f32[12,2,8,128]{3,2,1,0:T(8,128)S(1)} %get-tuple-element.191), channel_id=1, source_target_pairs={{0,6},{1,7},{2,4},{3,5},{4,2},{5,3},{6,0},{7,1},{8,14},{9,15},{10,... | collective-permute-start | bytes 294920 | tf_op jit(solution)/shard_map/cond/branch_3_fun/ppermute | solution.py:334
  109.4 6.1 %collective-permute-start.56 = (f32[12,2,8,128]{3,2,1,0:T(8,128)S(1)}, f32[12,2,8,128]{3,2,1,0:T(8,128)S(1)}, u32[]{:S(2)}, u32[]{:S(2)}) collective-permute-start(f32[12,2,8,128]{3,2,1,0:T(8,128)S(1)} %get-tuple-element.192), channel_id=1, source_target_pairs={{0,7},{1,6},{2,5},{3,4},{4,3},{5,2},{6,1},{7,0},{8,15},{9,14},{10,... | collective-permute-start | bytes 294920 | tf_op jit(solution)/shard_map/cond/branch_3_fun/ppermute | solution.py:334
  112.2 5.3 %collective-permute-start.57 = (f32[12,2,8,128]{3,2,1,0:T(8,128)S(1)}, f32[12,2,8,128]{3,2,1,0:T(8,128)S(1)}, u32[]{:S(2)}, u32[]{:S(2)}) collective-permute-start(f32[12,2,8,128]{3,2,1,0:T(8,128)S(1)} %get-tuple-element.193), channel_id=1, source_target_pairs={{0,2},{1,3},{2,0},{3,1},{4,6},{5,7},{6,4},{7,5},{8,10},{9,11},{10,... | collective-permute-start | bytes 294920 | tf_op jit(solution)/shard_map/cond/branch_3_fun/ppermute | solution.py:334
  113.0 6.7 %collective-permute-start.58 = (f32[12,2,8,128]{3,2,1,0:T(8,128)S(1)}, f32[12,2,8,128]{3,2,1,0:T(8,128)S(1)}, u32[]{:S(2)}, u32[]{:S(2)}) collective-permute-start(f32[12,2,8,128]{3,2,1,0:T(8,128)S(1)} %get-tuple-element.194), channel_id=1, source_target_pairs={{0,3},{1,2},{2,1},{3,0},{4,7},{5,6},{6,5},{7,4},{8,11},{9,10},{10,... | collective-permute-start | bytes 294920 | tf_op jit(solution)/shard_map/cond/branch_3_fun/ppermute | solution.py:334
  114.5 5.1 %collective-permute-start.59 = (f32[12,2,8,128]{3,2,1,0:T(8,128)S(1)}, f32[12,2,8,128]{3,2,1,0:T(8,128)S(1)}, u32[]{:S(2)}, u32[]{:S(2)}) collective-permute-start(f32[12,2,8,128]{3,2,1,0:T(8,128)S(1)} %get-tuple-element.195), channel_id=1, source_target_pairs={{0,1},{1,0},{2,3},{3,2},{4,5},{5,4},{6,7},{7,6},{8,9},{9,8},{10,11... | collective-permute-start | bytes 294920 | tf_op jit(solution)/shard_map/cond/branch_3_fun/ppermute | solution.py:334
  (5 other events, 14.4 us)
